TPU v7x, 32 devices: a whole 2x2x4 slice. The times are simulated.
32 devices in a mesh: wide: 8 (over y, x, core), narrow: 4 (over z).
Axes of the slice: x: 2, y: 2, z: 4, core: 2. Of those that a mesh axis runs over, the one named last changes fastest.
Arguments:
- tokens: bfloat16 [32, 1536, 768], P(('wide', 'narrow')), may hold values from -6 to 6
- lengths: int32 [8, 4], P('wide'), may hold values from 1 to 1536, 4608 in all within a row
- qkv_weight: bfloat16 [768, 3, 768], P(None, None, 'narrow'), may hold values from -0.3125 to 0.3125
- qkv_bias: bfloat16 [3, 768], P(None, 'narrow'), may hold values from -3 to 3
- out_weight: bfloat16 [768, 768], P('narrow'), may hold values from -2.5 to 2.5
- out_bias: bfloat16 [768], replicated, may hold values from -2 to 2
- norm1_gain: bfloat16 [768], replicated, may hold values from 0.099609375 to 1.8984375
- norm1_shift: bfloat16 [768], replicated, may hold values from -2 to 2
- up_weight: bfloat16 [768, 3072], P(None, 'narrow'), may hold values from -0.21875 to 0.21875
- up_bias: bfloat16 [3072], P('narrow'), may hold values from -2 to 2
- down_weight: bfloat16 [3072, 768], P('narrow'), may hold values from -0.109375 to 0.109375
- down_bias: bfloat16 [768], replicated, may hold values from -2 to 2
- norm2_gain: bfloat16 [768], replicated, may hold values from 0.099609375 to 1.8984375
- norm2_shift: bfloat16 [768], replicated, may hold values from -2 to 2
- cotangent: bfloat16 [32, 1536, 768], P(('wide', 'narrow')), may hold values from -6 to 6
Outputs:
- output: bfloat16 [32, 1536, 768], P(('wide', 'narrow'))
- input_grad: float32 [32, 1536, 768], P(('wide', 'narrow'))
- grad_qkv_weight: float32 [768, 3, 768], P(None, None, 'narrow')
- grad_qkv_bias: float32 [3, 768], P(None, 'narrow')
- grad_out_weight: float32 [768, 768], P('narrow')
- grad_out_bias: float32 [768], replicated
- grad_norm1_gain: float32 [768], replicated
- grad_norm1_shift: float32 [768], replicated
- grad_up_weight: float32 [768, 3072], P(None, 'narrow')
- grad_up_bias: float32 [3072], P('narrow')
- grad_down_weight: float32 [3072, 768], P('narrow')
- grad_down_bias: float32 [768], replicated
- grad_norm2_gain: float32 [768], replicated
- grad_norm2_shift: float32 [768], replicated
Inputs may be any that keep to these rules, and one draw needn't show every extreme that they name: The 4 lengths of each wide index sum to 4608; positions at or beyond a slot's length are keys that no query attends to.
All inputs are finite; a program needn't handle non-finite values.
Results may differ from a plain program's by a relative error of at most 0.018.
The roundings to bfloat16 on the way count: a program that leaves them out, or rounds other values in their place, can miss the bound.
Values may be sent and summed in bfloat16 or wider, within the bound.
No kernel may reach another device: no remote copies, remote signals or barrier semaphores. Data moves between devices by JAX's collectives and lax.ppermute only.
A program may use at most 256 MiB of HBM per device.

v0:
```python
import functools

import jax
import jax.numpy as jnp
from jax import lax
from jax.experimental import pallas as pl
from jax.experimental.pallas import tpu as pltpu
from jax.sharding import PartitionSpec as P

bf = jnp.bfloat16
f32 = jnp.float32
LOG2E = 1.4426950408889634
HEADS = 12
HD = 64
SPLIT = 8
EXTRA = 8
MIB = 1 << 20


def dg(a, b, ca, cb):
    return lax.dot_general(a, b, (((ca,), (cb,)), ((), ())), preferred_element_type=f32)


def mean(x):
    return jnp.mean(x, axis=-1, keepdims=True)


def shape(s, d):
    return jax.ShapeDtypeStruct(s, d)


SMEM = pl.BlockSpec(memory_space=pltpu.SMEM)
ANY = pl.BlockSpec(memory_space=pl.ANY)


def length_of(lengths):
    return lengths[0, lax.axis_index("narrow")]


def low_bits():
    return jnp.bitwise_and(lax.axis_index("wide"), SPLIT - 1)


def params(mib):
    return pltpu.CompilerParams(vmem_limit_bytes=mib * MIB)


def cost(flops, nbytes):
    return pl.CostEstimate(flops=1, bytes_accessed=1, transcendentals=0)


def put_piece(meta, src, g, lanes, place, dst, sem):
    rel, half, whole = place
    rows = src.shape[1]
    at = 0 if rel is None else (low_bits() ^ rel) * whole + half
    return pltpu.make_async_copy(src.at[g, :, lanes], dst.at[pl.ds(pl.multiple_of(at, 16), rows), :], sem)


def attn_fwd_kernel(meta, *refs, C, KC, G, layout, own):
    pieces, refs = refs[:len(layout)], refs[len(layout):]
    x, b, cos, sin, q_t, k_t, v_d, e, ctx, linv, w_t, *rest = refs
    if own:
        x_t, Q2, KD, VA, S, W, flag, sem = rest
    else:
        x_t, (Q2, KD, VA, S, W, flag, sem) = x, rest
    h = pl.program_id(0)
    length = length_of(meta)

    if own:
        @pl.when(h == 0)
        def _():
            x_t[...] = x[...].T
            n = pieces[0].shape[0]
            w_t[:n, :] = pieces[0][...]
            w_t[n:, :] = pieces[1][...]
    else:
        groups = pieces[0].shape[0]

        def copies(g):
            return [put_piece(meta, pieces[t], g, slice(None), layout[t], W.at[g], sem.at[g, t]) for t in range(len(pieces))]

        @pl.when(h == 0)
        def _():
            for g in range(groups):
                for c in copies(g):
                    c.start()

        @pl.when(lax.rem(h, G) == 0)
        def _():
            g = lax.div(h, G)
            for c in copies(g):
                c.wait()
            w_t[...] = W[g].T

    at = lax.rem(h, G)
    w = jnp.concatenate([w_t[pl.ds(pl.multiple_of((p * G + at) * HD, HD), HD), :] for p in range(3)], axis=0)
    bias = [jnp.broadcast_to(b[i:i + 1, :], (2 * HD, HD)).T[:, :1] for i in range(3)]
    p = dg(w, x_t[...], 1, 0) + jnp.concatenate(bias, axis=0)
    c, d = cos[...], sin[...]

    def rot(v):
        u, z = v[:HD // 2], v[HD // 2:]
        return jnp.concatenate([u * c - z * d, z * c + u * d], axis=0)

    live = lax.broadcasted_iota(jnp.int32, (HD, C), 1) < length
    q = rot(p[:HD]).astype(bf).astype(f32)
    k = jnp.where(live, rot(p[HD:2 * HD]), 0.0).astype(bf)
    v = jnp.where(live, p[2 * HD:], 0.0).astype(bf)
    q_t[...] = (q * 0.125).astype(bf)
    q = q * (0.125 * LOG2E)
    hi = q.astype(bf)
    Q2[:HD, :] = hi
    Q2[HD:, :] = (q - hi.astype(f32)).astype(bf)
    k_t[...] = k
    KD[...] = jnp.concatenate([k, k], axis=0).T
    v_d[...] = jnp.concatenate([v, v], axis=0).T
    VA[:HD, :] = v
    VA[HD:, :] = jnp.where(live[:16], 1.0, 0.0).astype(bf)
    kf = k.astype(f32)
    qn = jnp.max(jnp.sum(q * q, axis=0, keepdims=True))
    kn = jnp.max(jnp.sum(kf * kf, axis=0, keepdims=True))
    flag[0] = (qn * kn <= 1e4).astype(jnp.int32)

    @pl.when(flag[0] == 1)
    def _():
        for j in range(C // KC):
            r = slice(j * KC, (j + 1) * KC)
            e[r, :] = jnp.exp2(dg(KD[r, :], Q2[...], 1, 0)).astype(bf)

    @pl.when(flag[0] == 0)
    def _():
        BQ = S.shape[1]

        def block(i, carry):
            cols = pl.ds(pl.multiple_of(i * BQ, BQ), BQ)

            def score(j, m):
                r = pl.ds(pl.multiple_of(j * KC, KC), KC)
                keys = lax.broadcasted_iota(jnp.int32, (KC, BQ), 0) + j * KC
                x = jnp.where(keys < length, dg(KD[r, :], Q2[:, cols], 1, 0), -1e30)
                S[r, :] = x
                return jnp.maximum(m, jnp.max(x, axis=0, keepdims=True))

            m = lax.fori_loop(0, C // KC, score, jnp.full((1, BQ), -1e30, f32))

            def power(j, carry):
                r = pl.ds(pl.multiple_of(j * KC, KC), KC)
                e[r, cols] = jnp.exp2(S[r, :] - m).astype(bf)
                return carry

            return lax.fori_loop(0, C // KC, power, carry)

        lax.fori_loop(0, C // BQ, block, 0)

    o = dg(VA[...], e[...], 1, 0)
    inv = 1.0 / o[HD:HD + 1]
    linv[...] = inv
    ctx[...] = (o[:HD] * inv).astype(bf)


def attn_fwd(meta, pieces, layout, x, b, cos, sin, own):
    groups, _, D = pieces[0].shape if not own else (1,) + pieces[0].shape
    C = x.shape[0] if own else x.shape[1]
    G = b.shape[1]
    H = groups * G
    at = lambda h: (h, 0, 0)
    fix = lambda a: pl.BlockSpec(a.shape, lambda h: (0,) * a.ndim, pipeline_mode=pl.Buffered(1))
    hb = pl.BlockSpec((None, HD, C), at)
    out_specs = [hb, hb, pl.BlockSpec((None, C, 2 * HD), at), pl.BlockSpec((None, C, C), at), hb,
                 pl.BlockSpec((None, 1, C), at), pl.BlockSpec((None, D, D), lambda h: (h // G, 0, 0))]
    out_shape = [shape((H, HD, C), bf), shape((H, HD, C), bf), shape((H, C, 2 * HD), bf), shape((H, C, C), bf),
                 shape((H, HD, C), bf), shape((H, 1, C), f32), shape((groups, D, D), bf)]
    if own:
        out_specs.append(pl.BlockSpec((D, C), lambda h: (0, 0)))
        out_shape.append(shape((D, C), bf))
    return pl.pallas_call(
        functools.partial(attn_fwd_kernel, C=C, KC=min(128, C), G=G, layout=layout, own=own), grid=(H,),
        in_specs=[SMEM] + ([fix(p) for p in pieces] if own else [ANY] * len(pieces))
        + [fix(x), pl.BlockSpec((None, None, 3, HD), lambda h: (h // G, h % G, 0, 0)), fix(cos), fix(sin)],
        out_specs=out_specs, out_shape=out_shape,
        scratch_shapes=[pltpu.VMEM((2 * HD, C), bf), pltpu.VMEM((C, 2 * HD), bf), pltpu.VMEM((HD + 16, C), bf),
                        pltpu.VMEM((C, C // 3 if C % 384 == 0 else C), f32), pltpu.VMEM((8, 128) if own else (groups, D, D), bf),
                        pltpu.SMEM((1,), jnp.int32), pltpu.SemaphoreType.DMA((groups, len(pieces)))],
        compiler_params=params(60), cost_estimate=cost(H * (4 * C * C * 256 + 2 * C * D * 3 * HD), H * C * C * 2 + 8 * MIB),
        name="attn_fwd_own" if own else "attn_fwd",
    )(meta, *pieces, x, b, cos, sin)


def ffn_kernel(meta, u_own, d_own, *refs, R, layout):
    pieces, refs = refs[:len(layout)], refs[len(layout):]
    tok, cot, *refs = refs
    J = pieces[0].shape[0] + 1
    ctxs, ows, refs = refs[:2], refs[2:4], refs[4:]
    (vec, ub, out, act, gu, hid_t, gl_t, g1_o, gol_t, do_t, small, ubg, G, U, Dn, sem) = refs
    i = pl.program_id(0)
    groups = J - 1

    def copies():
        cs = [pltpu.make_async_copy(u_own, U.at[0], sem.at[0, 0, 0]), pltpu.make_async_copy(d_own, Dn.at[0], sem.at[1, 0, 0])]
        for g in range(groups):
            for t, (piece, (parts, place)) in enumerate(zip(pieces, layout)):
                for k, s in enumerate(parts):
                    lanes = slice(k * U.shape[2], (k + 1) * U.shape[2])
                    cs.append(put_piece(meta, piece, g, lanes, place, (U, Dn)[s].at[g + 1], sem.at[s, g + 1, t]))
        return cs

    @pl.when(i == 0)
    def _():
        for c in copies():
            c.start()
        small[...] = jnp.zeros_like(small)
        ubg[...] = jnp.zeros_like(ubg)

    ob, g1, s1, db, g2, s2 = [vec[k:k + 1, :] for k in range(6)]
    D = tok.shape[1]
    F = U.shape[2]

    def csum(k, x):
        small[k:k + 1, :] += jnp.sum(x, axis=0, keepdims=True)

    ow = jnp.concatenate([w[g] for w in ows for g in range(w.shape[0])], axis=0)
    ctx = jnp.concatenate([c[...].reshape(-1, R) for c in ctxs], axis=0)
    pre = tok[...].astype(f32) + dg(ctx.T, ow, 1, 0) + ob
    cen = pre - mean(pre)
    r1 = lax.rsqrt(mean(cen * cen) + 1e-6)
    n1 = cen * r1
    hid = n1 * g1 + s1
    hl = hid.astype(bf)
    hid_t[...] = hl.T
    acc = hid + db

    @pl.when(i == 0)
    def _():
        for c in copies():
            c.wait()

    for j in range(J):
        u = dg(hl, U[j], 1, 0) + ub[j:j + 1, :]
        phi = 0.5 * lax.erf(u * 0.7071067811865476) + 0.5
        a = (u * phi).astype(bf)
        act[:, j * F:(j + 1) * F] = a
        G[:, j * F:(j + 1) * F] = phi + u * (jnp.exp2(u * u * -0.7213475204444817) * 0.3989422804014327)
        acc = acc + dg(a, Dn[j], 1, 0)
    cen = acc - mean(acc)
    r2 = lax.rsqrt(mean(cen * cen) + 1e-6)
    n2 = cen * r2
    out[...] = (n2 * g2 + s2).astype(bf)
    c = cot[...].astype(f32)
    csum(0, c * n2)
    csum(1, c)
    sg = c * g2
    gt = r2 * (sg - mean(sg) - n2 * mean(sg * n2))
    csum(2, gt)
    gl = gt.astype(bf)
    gl_t[...] = gl.T
    dh = gt
    for j in range(J):
        g = dg(gl, Dn[j], 1, 1) * G[:, j * F:(j + 1) * F]
        ubg[j:j + 1, :] += jnp.sum(g, axis=0, keepdims=True)
        gb = g.astype(bf)
        gu[:, j * F:(j + 1) * F] = gb
        dh = dh + dg(gb, U[j], 1, 1)
    csum(3, dh * n1)
    csum(4, dh)
    sg = dh * g1
    go = r1 * (sg - mean(sg) - n1 * mean(sg * n1))
    csum(5, go)
    g1_o[...] = go
    gol = go.astype(bf)
    gol_t[...] = gol.T
    do_t[...] = dg(ow, gol, 1, 1).astype(bf).reshape(do_t.shape)


def ffn(meta, u_own, d_own, pieces, layout, tok, cot, ctxs, wts, vec, ub, R=512):
    C, D = tok.shape
    J, F = ub.shape
    H = HEADS
    row = lambda w: pl.BlockSpec((R, w), lambda i: (i, 0))
    col = pl.BlockSpec((D, R), lambda i: (0, i))
    fix = lambda a: pl.BlockSpec(a.shape, lambda i: (0,) * a.ndim, pipeline_mode=pl.Buffered(1))
    hb = lambda n: pl.BlockSpec((n, HD, R), lambda i: (0, 0, i))
    acc = lambda s: pl.BlockSpec(s, lambda i: (0, 0))
    share = H // J * HD
    at = 3
    owb = lambda w: pl.BlockSpec((w.shape[0], share, D), lambda i: (0, at, 0), pipeline_mode=pl.Buffered(1))
    return pl.pallas_call(
        functools.partial(ffn_kernel, R=R, layout=layout), grid=(C // R,),
        in_specs=[SMEM, ANY, ANY] + [ANY] * len(pieces) + [row(D), row(D)] + [hb(c.shape[0]) for c in ctxs] + [owb(w) for w in wts] + [fix(vec), fix(ub)],
        out_specs=[row(D), row(J * F), row(J * F), col, col, row(D), col, hb(H), acc((8, D)), acc((J, F))],
        out_shape=[shape((C, D), bf), shape((C, J * F), bf), shape((C, J * F), bf), shape((D, C), bf), shape((D, C), bf), shape((C, D), f32),
                   shape((D, C), bf), shape((H, HD, C), bf), shape((8, D), f32), shape((J, F), f32)],
        scratch_shapes=[pltpu.VMEM((R, J * F), f32), pltpu.VMEM((J, D, F), bf), pltpu.VMEM((J, F, D), bf),
                        pltpu.SemaphoreType.DMA((2, J, len(pieces)))],
        compiler_params=params(60), cost_estimate=cost(2 * C * D * (2 * D + 4 * J * F), 60 * MIB), name="ffn",
    )(meta, u_own, d_own, *pieces, tok, cot, *ctxs, *wts, vec, ub)


def attn_bwd_kernel(meta, e, v_d, do_t, ctx, linv, q_t, k_t, cos, sin, gp, gb, D2, DI, DS, DST, ET, *, C, KC):
    length = length_of(meta)
    g = do_t[...].astype(f32)
    inv = linv[...]
    DI[...] = jnp.sum(g * ctx[...].astype(f32), axis=0, keepdims=True) * inv
    g = g * inv
    hi = g.astype(bf)
    D2[:HD, :] = hi
    D2[HD:, :] = (g - hi.astype(f32)).astype(bf)
    for j in range(C // KC):
        r = slice(j * KC, (j + 1) * KC)
        dp = dg(v_d[r, :], D2[...], 1, 0)
        ej = e[r, :]
        ds = (ej.astype(f32) * (dp - DI[...])).astype(bf)
        DS[r, :] = ds
        DST[:, r] = ds.T
        ET[:, r] = ej.T
    dq = dg(k_t[...], DS[...], 1, 0)
    dk = dg(q_t[...], DST[...], 1, 0)
    dv = dg(D2[:HD, :], ET[...], 1, 0)
    live = lax.broadcasted_iota(jnp.int32, (HD, C), 1) < length
    c, s = cos[...], sin[...]

    def unrot(x):
        u, w = x[:HD // 2], x[HD // 2:]
        return jnp.concatenate([u * c + w * s, w * c - u * s], axis=0)

    def put(k, x):
        gp[k] = x.astype(bf)
        total = jnp.sum(x, axis=1, keepdims=True)
        gb[k:k + 1, :] = jnp.broadcast_to(total, (HD, 2 * HD)).T[:1]

    put(0, unrot(dq * 0.125))
    put(1, unrot(jnp.where(live, dk, 0.0)))
    put(2, jnp.where(live, dv, 0.0))


def attn_bwd(meta, saved, do_t, cos, sin, G, first, shift, H):
    e, v_d, ctx, linv, q_t, k_t = saved
    C = e.shape[1]
    sp = lambda s: pl.BlockSpec((None,) + s, lambda h: (h + first, 0, 0))
    tab = pl.BlockSpec((HD // 2, C), lambda h: (0, 0))
    return pl.pallas_call(
        functools.partial(attn_bwd_kernel, C=C, KC=min(256, C)), grid=(H,),
        in_specs=[SMEM, sp((C, C)), sp((C, 2 * HD)), pl.BlockSpec((None, HD, C), lambda h: (h + first + shift, 0, 0)), sp((HD, C)), sp((1, C)),
                  sp((HD, C)), sp((HD, C)), tab, tab],
        out_specs=[pl.BlockSpec((None, 3, None, HD, C), lambda h: (h // G, 0, h % G, 0, 0)), pl.BlockSpec((None, 3, HD), lambda h: (h, 0, 0))],
        out_shape=[shape((H // G, 3, G, HD, C), bf), shape((H, 3, HD), f32)],
        scratch_shapes=[pltpu.VMEM((2 * HD, C), bf), pltpu.VMEM((1, C), f32)] + [pltpu.VMEM((C, C), bf)] * 3,
        compiler_params=params(60), cost_estimate=cost(H * 8 * C * C * 256, H * C * C * 2 + 16 * MIB), name="attn_bwd",
    )(meta, e, v_d, do_t, ctx, linv, q_t, k_t, cos, sin)


NEAR = (0, 2, 4, 6)
SWAP = (0, 4, 2, 6)


def lay(meta, S, theirs, mine, rows, lanes, order):
    for i, rel in enumerate(order):
        for ref, low in ((mine, 0), (theirs, 1)):
            ref[i // 2, i % 2, 0, rows, lanes] = S[low_bits() ^ (rel | low)].astype(bf)


def wgrad_d_kernel(meta, gl_t, act, vecs, theirs, mine, S):
    rows = S.shape[1]
    S[...] = dg(gl_t[...], act[...], 1, 0).reshape(S.shape)
    lay(meta, S, theirs, mine, slice(0, rows), slice(None), SWAP)
    for i, rel in enumerate(SWAP):
        for ref, low in ((mine, 0), (theirs, 1)):
            line = vecs[pl.ds(low_bits() ^ (rel | low), 1), :]
            ref[i // 2, i % 2, 0, rows:, :] = jnp.broadcast_to(line, (EXTRA, line.shape[1])).astype(bf)


def wgrad_u_kernel(meta, hid_t, gu, gol_t, *refs):
    c0, c1, theirs, mine, S, SO = refs
    F = gu.shape[1]
    S[...] = dg(hid_t[...], gu[...], 1, 0).reshape(S.shape)
    lay(meta, S, theirs, mine, slice(None), slice(0, F), NEAR)

    def out(ctx):
        SO[...] = dg(gol_t[...], ctx[...].reshape(-1, ctx.shape[-1]), 1, 1).reshape(SO.shape)

    pl.when(pl.program_id(0) == 0)(lambda: out(c0))
    pl.when(pl.program_id(0) > 0)(lambda: out(c1))
    lay(meta, SO, theirs, mine, slice(None), slice(F, F + SO.shape[2]), NEAR)


def wgrad_q_kernel(meta, tok_t, *refs):
    gps, (gb, theirs, mine, S) = refs[:-4], refs[-4:]
    rows = S.shape[1]
    if len(gps) == 1:
        S[...] = dg(tok_t[...], gps[0][...], 1, 1).reshape(S.shape)
    for j, gp in enumerate(gps if len(gps) > 1 else ()):
        @pl.when(pl.program_id(0) == j)
        def _(gp=gp):
            S[...] = dg(tok_t[...], gp[...], 1, 1).reshape(S.shape)

    lay(meta, S, theirs, mine, slice(0, rows), slice(None), SWAP)
    line = jnp.broadcast_to(gb[...], (EXTRA, gb.shape[1])).astype(bf)
    for i in range(4):
        for ref in (mine, theirs):
            ref[i // 2, i % 2, 0, rows:, :] = line


def wgrad(kernel, meta, args, specs, J, rows, lanes, scratch, name, flops):
    spec = pl.BlockSpec((2, 2, 1, rows, lanes), lambda j: (0, 0, j, 0, 0))
    return pl.pallas_call(
        kernel, grid=(J,), in_specs=[SMEM] + specs, out_specs=[spec] * 2, out_shape=[shape((2, 2, J, rows, lanes), bf)] * 2,
        scratch_shapes=[pltpu.VMEM(s, f32) for s in scratch],
        compiler_params=params(28), cost_estimate=cost(flops, 20 * MIB), name=name,
    )(meta, *[pltpu.with_memory_space_constraint(x, pltpu.HBM) for x in args])


def final_du_kernel(meta, x, y, down, up, ow, small, S, SO):
    rows = S.shape[1]
    F = up.shape[1]
    for low, ref in enumerate((x, y)):
        for t, rel in enumerate(NEAR):
            at = low_bits() ^ (rel | low)
            S[at] = ref[t, :rows, :F].astype(f32)
            small[pl.ds(at, 1), :] = ref[t, rows:rows + 1, :F].astype(f32)
            up[pl.ds(pl.multiple_of(at * rows, rows), rows), :] = ref[t, :rows, F:2 * F].astype(f32)
            SO[at] = ref[t, :rows, 2 * F:].astype(f32)
    down[...] = S[...].reshape(down.shape).T
    ow[...] = SO[...].reshape(-1, SO.shape[2]).T


def final_q_kernel(meta, x, y, qkv, gb, S):
    rows = x.shape[1] - EXTRA
    for low, ref in enumerate((x, y)):
        for t, rel in enumerate(NEAR):
            S[low_bits() ^ (rel | low)] = ref[t, :rows, :].astype(f32)
    qkv[...] = S[...].reshape(-1, S.shape[2]).T
    gb[...] = x[0, rows:rows + 1, :].astype(f32)


def final(kernel, meta, xs, outs, scratch, name):
    return pl.pallas_call(
        kernel, in_specs=[SMEM] + [pl.BlockSpec(memory_space=pltpu.VMEM)] * 2,
        out_shape=[shape(s, f32) for s in outs], scratch_shapes=[pltpu.VMEM(s, f32) for s in scratch],
        compiler_params=params(60), cost_estimate=cost(0, 8 * MIB), name=name,
    )(meta, *xs)


def input_grad_kernel(*refs, N, n):
    gps, (w0, w1, g1, *_, out) = refs[:n], refs[n:]
    acc = g1[...]
    j = 0
    for gp in gps:
        for i in range(gp.shape[0]):
            w = w0[0, :N, :] if j == 0 else w1[j - 1, :N, :]
            acc = acc + dg(gp[i], w, 0, 0)
            j += 1
    out[...] = acc


def input_grad(gps, w0, w1, g1, first, count, before=None, R=256):
    _, N, C = gps[0].shape
    D = g1.shape[1]
    fix = lambda a: pl.BlockSpec(a.shape, lambda i: (0,) * a.ndim, pipeline_mode=pl.Buffered(1))
    row = pl.BlockSpec((R, D), lambda i: (i + first, 0))
    more = [] if before is None else [before]
    return pl.pallas_call(
        functools.partial(input_grad_kernel, N=N, n=len(gps)), grid=(count,),
        in_specs=[pl.BlockSpec((g.shape[0], N, R), lambda i: (0, 0, i + first)) for g in gps] + [fix(w0), fix(w1), row] + [ANY] * len(more),
        out_specs=row, out_shape=shape((C, D), f32), input_output_aliases={len(gps) + 3: 0} if more else {},
        compiler_params=params(28), cost_estimate=cost(2 * C * D * D * 3, 24 * MIB), name="input_grad",
    )(*gps, w0, w1, g1, *more)


def fetch(x, s):
    n = lax.axis_size("narrow")
    return lax.ppermute(x, "narrow", [((i + s) % n, i) for i in range(n)])


def give(x, s):
    n = lax.axis_size("narrow")
    return lax.ppermute(x, "narrow", [(i, (i + s) % n) for i in range(n)])


def flip(x, bit):
    return lax.ppermute(x, "wide", [(i, i ^ bit) for i in range(lax.axis_size("wide"))])


def total(terms):
    x = terms[0].astype(f32)
    for y in terms[1:]:
        x = x + y.astype(f32)
    return x.astype(bf)


def rest(x):
    bit = SPLIT
    while bit < lax.axis_size("wide"):
        x = add(x, flip(x, bit))
        bit *= 2
    return x


def tie(xs, deps):
    return lax.optimization_barrier((xs, deps))[0]


def add(a, b):
    return (a.astype(f32) + b.astype(f32)).astype(bf)


def rotary_tables(capacity):
    positions = jnp.arange(capacity).astype(f32)
    frequencies = 10000.0 ** (-2.0 * jnp.arange(HD // 2).astype(f32) / HD)
    angles = frequencies[:, None] * positions[None, :]
    return jnp.cos(angles), jnp.sin(angles)


def shards(
    tokens, lengths, qkv_weight, qkv_bias, out_weight, out_bias, norm1_gain, norm1_shift,
    up_weight, up_bias, down_weight, down_bias, norm2_gain, norm2_shift, cotangent,
):
    J = lax.axis_size("narrow")
    tok, cot = tokens[0], cotangent[0]
    C, D = tok.shape
    G = HEADS // J
    N = 3 * G * HD
    F = up_weight.shape[1]
    rows = D // SPLIT
    low = jnp.bitwise_and(lax.axis_index("wide"), SPLIT - 1).astype(jnp.int32)
    meta = lengths
    cos, sin = rotary_tables(C)

    qkv_t = qkv_weight.transpose(1, 2, 0).reshape(N, D)
    qo = jnp.concatenate([qkv_weight.reshape(D, N), out_weight.T], axis=1)
    bias = jnp.concatenate([qkv_bias.reshape(-1), up_bias])
    bias = jnp.pad(bias, (0, 2 * D - bias.size)).reshape(2, D)
    cut = lambda x: lax.dynamic_slice_in_dim(x, low * rows, rows, 0)
    q_piece = jnp.concatenate([cut(qo), jnp.pad(bias, ((0, EXTRA - 2), (0, 0)))], axis=0)
    got = [fetch(q_piece, s) for s in range(1, J)]
    vec = jnp.stack([out_bias, norm1_gain, norm1_shift, down_bias, norm2_gain, norm2_shift]).astype(f32)
    b_own = qkv_bias.astype(f32).reshape(1, 3, G, HD).transpose(0, 2, 1, 3)
    ud_piece = jnp.concatenate([cut(up_weight), cut(down_weight)], axis=1)
    ud_got = [fetch(tie(ud_piece, q_piece), 1)]
    q0, k0, v0, e0, c0, l0, wt0, tok_t = attn_fwd(meta, [qkv_t, out_weight], (0, 1), tok, b_own, cos, sin, True)
    got, ud_got, tok_t = lax.optimization_barrier((got, ud_got, tok_t))
    biases = jnp.stack([bias] + [x[rows:rows + 2] for x in got]).reshape(J, 2 * D).astype(f32)
    bq, ub = biases[1:, :N].reshape(J - 1, 3, G, HD).transpose(0, 2, 1, 3), biases[:, N:N + F]
    q = jnp.stack([x[:rows] for x in got])
    q_near = [flip(q, rel) for rel in NEAR[1:]]
    ud_2, ud_3 = [fetch(tie(ud_piece, got), n) for n in (2, 3)]
    q_near, ud_2, ud_3, bq, ub, vec = lax.optimization_barrier((q_near, ud_2, ud_3, bq, ub, vec))
    q_near = [q] + q_near
    q_far = [flip(x, 1) for x in q_near]
    q_places = tuple((rel | low, 0, rows) for low in (0, 1) for rel in NEAR)
    q_far, ud_2, ud_3 = lax.optimization_barrier((q_far, ud_2, ud_3))
    ud = jnp.stack(ud_got + [ud_2, ud_3])
    q_pieces = q_near + q_far
    ud_near = [flip(ud, rel) for rel in NEAR[1:]]
    ud_far = [flip(ud, 1)]
    tok_t = tie(tok_t, ud)
    q1, k1, v1, e1, c1, l1, wt1 = attn_fwd(meta, q_pieces, q_places, tok_t, bq, cos, sin, False)
    ud_near, ud_far, c1 = lax.optimization_barrier((ud_near, ud_far, c1))
    ud_pieces = [ud] + ud_near + ud_far + [flip(x, 1) for x in ud_near]
    ud_places = [(rel | low, 0, rows) for low in (0, 1) for rel in NEAR]
    ud_layout = tuple(((0, 1), place) for place in ud_places)
    out, act, gu, hid_t, gl_t, g1, gol_t, do_t, small, ubg = ffn(
        meta, up_weight, down_weight, ud_pieces, ud_layout, tok, cot, (c0, c1), (wt0, wt1), vec, ub)

    whole = lambda a: pl.BlockSpec(a.shape, lambda j: (0,) * a.ndim, pipeline_mode=pl.Buffered(1))
    vecs = jnp.concatenate([jnp.broadcast_to(small[None, :6], (J, 6, D)), ubg[:, None], jnp.zeros((J, 1, D), f32)], axis=1)
    u_t, u_m = wgrad(
        wgrad_u_kernel, meta, (hid_t, gu, gol_t, c0, c1),
        [whole(hid_t), pl.BlockSpec((C, F), lambda j: (0, j)), whole(gol_t), pl.BlockSpec((G, HD, C), lambda j: (0, 0, 0)),
         pl.BlockSpec((G, HD, C), lambda j: (jnp.maximum(j - 1, 0), 0, 0))],
        J, rows, F + G * HD, [(SPLIT, rows, F), (SPLIT, rows, G * HD)], "wgrad_u", 2 * C * D * (J * F + D))
    u_1 = flip(u_t, 1)
    gl_t = tie(gl_t, u_t)
    d_t, d_m = wgrad(
        wgrad_d_kernel, meta, (gl_t, act, vecs),
        [whole(gl_t), pl.BlockSpec((C, F), lambda j: (0, j)), pl.BlockSpec((None, 8, D), lambda j: (j, 0, 0))],
        J, rows + EXTRA, F, [(SPLIT, rows, F)], "wgrad_d", 2 * C * D * J * F)

    def grad_q(gps, gb):
        n = gb.shape[0]
        one = pl.BlockSpec((None, N, C), lambda j: (j, 0, 0)) if len(gps) == 1 else pl.BlockSpec((None, N, C), lambda j: (0, 0, 0))
        return wgrad(
            wgrad_q_kernel, meta, (tok_t, *gps, gb), [whole(tok_t)] + [one] * len(gps) + [pl.BlockSpec((None, 1, N), lambda j: (j, 0, 0))],
            n, rows + EXTRA, N, [(SPLIT, rows, N)], "wgrad_q", 2 * C * D * n * N)

    def backward(group, count, do_t):
        saved, shift = ((e0, v0, c0, l0, q0, k0), 0) if group == 0 else ((e1, v1, c1, l1, q1, k1), G)
        gp, gb = attn_bwd(meta, saved, do_t, cos, sin, G, group * G - shift, shift, count * G)
        return gp.reshape(count, N, C), gb.reshape(count, G, 3, HD).transpose(0, 2, 1, 3).reshape(count, 1, N)

    def first(terms):
        return total([t[1] for t in terms]), [t[0] for t in terms]

    u_1, u_m, d_t = lax.optimization_barrier((u_1, u_m, d_t))
    d_1 = flip(d_t, 1)
    u_s, u_k = first([u_m, u_1])
    u_2 = flip(u_s, 4)
    do_t = tie(do_t, u_s)
    d_1, d_m, do_t = lax.optimization_barrier((d_1, d_m, do_t))
    d_s, d_k = first([d_m, d_1])
    d_2 = flip(d_s, 2)
    do_t = tie(do_t, d_s)
    gpa, gba = backward(1, 2, do_t)
    u_2, d_2, gpa, do_t = lax.optimization_barrier((u_2, d_2, gpa, do_t))
    u_s, u_k = first(u_k + [u_2])
    u_3 = flip(u_s, 2)
    d_s, d_k = first(d_k + [d_2])
    d_3 = flip(d_s, 4)
    gpa_ = tie(gpa, (u_s, d_s))
    qa_t, qa_m = grad_q((gpa_,), gba)
    qa_1 = flip(qa_t, 1)
    do_t = tie(do_t, qa_t)
    gpb, gbb = backward(0, 1, do_t)
    u_3, d_3, qa_1, gpb, do_t = lax.optimization_barrier((u_3, d_3, qa_1, gpb, do_t))
    du_s = [jnp.concatenate([total([t[j] for t in d_k + [d_3]]), jnp.pad(total([t[j] for t in u_k + [u_3]]), ((0, EXTRA), (0, 0)))], axis=1)
            for j in range(J)]
    du_3 = [give(du_s[s], s) for s in (1, 3)]
    qa_s, qa_k = first([qa_m, qa_1])
    qa_2 = flip(qa_s, 2)
    do_t = tie(do_t, (du_s, qa_s))
    gpc, gbc = backward(3, 1, do_t)
    du_3, qa_2, gpb, gpc = lax.optimization_barrier((du_3, qa_2, gpb, gpc))
    qa_s, qa_k = first(qa_k + [qa_2])
    qa_3 = flip(qa_s, 4)
    gpc_ = tie(gpc, qa_s)
    du_2 = give(tie(du_s[2], qa_s), 2)
    qb_t, qb_m = grad_q((gpb, gpc_), jnp.concatenate([gbb, gbc], axis=0))
    qb_1 = flip(qb_t, 1)
    qa_3, du_2, qb_t, qb_m = lax.optimization_barrier((qa_3, du_2, qb_t, qb_m))
    du = rest(total([du_s[0], du_2] + du_3))
    du_x, du_y = flip(du, 2), flip(du, 4)
    qa_s = [total([t[j] for t in qa_k + [qa_3]]) for j in range(2)]
    q_3 = [give(qa_s[0], 1), give(qa_s[1], 2)]
    g1 = tie(g1, (qb_t, qa_s, du))
    x_grad = input_grad([gpb, gpa, gpc], wt0, wt1, g1, 0, C // 768)
    qb_1, qb_m, q_3, x_grad = lax.optimization_barrier((qb_1, qb_m, q_3, x_grad))
    qb_s = [total([t[i // 2, i % 2] for t in (qb_m, qb_1)]) for i in range(1, 4)]
    qb_k = [t[0, 0] for t in (qb_m, qb_1)]
    qb_2 = [flip(x, rel) for x, rel in zip(qb_s, SWAP[1:])]
    g1, x_grad = tie((g1, x_grad), qb_s)
    x_grad = input_grad([gpb, gpa, gpc], wt0, wt1, g1, C // 768, C // 256 - C // 768, x_grad)
    qb_2, du_x, du_y, x_grad = lax.optimization_barrier((qb_2, du_x, du_y, x_grad))
    cut_at = du.shape[0] // 16 * 8
    du_d = [flip(du_y[:cut_at], 2), flip(du_x[cut_at:], 4)]
    qb = total(qb_k + qb_2)
    q_3.append(give(qb[1], J - 1))
    q_3, du_d = lax.optimization_barrier((q_3, du_d))
    q = rest(total([qb[0]] + q_3))
    q_4 = [flip(q, rel) for rel in NEAR[1:]]
    du = jnp.stack([du, du_x, du_y, jnp.concatenate(du_d, axis=0)])
    du_5 = flip(du, 1)
    q_4, du_5 = lax.optimization_barrier((q_4, du_5))
    q = jnp.stack([q] + q_4)
    q_5 = flip(q, 1)
    du = tie(du, q)
    down_g, up_g, ow_g, small = final(
        final_du_kernel, meta, (du, du_5), [(F, D), (D, F), (G * HD, D), (8, D)], [(SPLIT, rows, F), (SPLIT, rows, G * HD)], "final_du")
    q_5, down_g = lax.optimization_barrier((q_5, down_g))
    qkv_g, gb = final(final_q_kernel, meta, (q, q_5), [(N, D), (1, N)], [(SPLIT, rows, N)], "final_q")
    return (
        out[None], x_grad[None], qkv_g.reshape(3, G * HD, D).transpose(2, 0, 1), gb.reshape(3, G * HD), ow_g, small[5], small[3], small[4],
        up_g, small[6], down_g, small[2], small[0], small[1],
    )


def solution(mesh):
    rows = P(("wide", "narrow"), None, None)
    weights = (P(None, None, "narrow"), P(None, "narrow"), P("narrow", None), P(), P(), P(),
               P(None, "narrow"), P("narrow"), P("narrow", None), P(), P(), P())
    return jax.shard_map(
        shards, mesh=mesh, in_specs=(rows, P("wide", None)) + weights + (rows,),
        out_specs=(rows, rows) + weights, check_vma=False,
    )
```

profile of v0, /device:TPU:0, one launch (start us, length us, event | category | flops | bytes accessed | tf_op | source)
XLA Modules:
  0.0 452.1 jit_solution(8331087430376684546)
XLA Ops:
  0.7 1.6 copy.37
  2.8 5.1 %collective-permute-start = (bf16[104,768]{1,0:T(8,128)(2,1)S(1)}, bf16[104,768]{1,0:T(8,128)(2,1)S(1)}, u32[]{:S(2)}, u32[]{:S(2)}) collective-permute-start(bf16[104,768]{1,0:T(8,128)(2,1)S(1)} %fusion.34), channel_id=1, source_target_pairs={{1,0},{2,1},{3,2},{0,3},{5,4},{6,5},{7,6},{4,7},{9,8},{10,9},{11,1... | collective-permute-start | bytes 479240 | tf_op jit(solution)/shard_map/ppermute | solution.py:470
  7.9 1.0 collective-permute-start.2
  8.9 1.0 constant_dynamic-slice_fusion
  9.9 2.9 collective-permute-start.3
  12.8 1.5 multiply_sine_fusion
  15.0 36.2 %attn_fwd_own.1 = (bf16[3,64,1536]{2,1,0:T(8,128)(2,1)}, bf16[3,64,1536]{2,1,0:T(8,128)(2,1)}, bf16[3,1536,128]{2,1,0:T(8,128)(2,1)}, bf16[3,1536,1536]{2,1,0:T(...) custom-call(s32[1,4]{1,0:T(1,128)} %meta.23, ...), custom_call_target="tpu_custom_call" | custom-call | flops 1 | bytes 1 | tf_op jit(solution)/shard_map/attn_fwd_own/pallas_call | solution.py:176
  52.0 1.2 collective-permute-start.8
  53.4 1.6 collective-permute-start.5
  54.9 1.5 collective-permute-start.6
  58.4 14.3 %collective-permute-done.8 = bf16[96,1536]{1,0:T(8,128)(2,1)S(1)} collective-permute-done((bf16[96,1536]{1,0:T(8,128)(2,1)S(1)}, bf16[96,1536]{1,0:T(8,128)(2,1)S(1)}, u32[]{:S(2)}, u32[]{:S(2)}) %collective-permute-start.8) | collective-permute-done | bytes 294944 | tf_op jit(solution)/shard_map/ppermute | solution.py:470
  72.7 1.7 collective-permute-done.6.refs_2_
  75.1 1.2 collective-permute-done.10.refs_5_
  78.5 1.5 collective-permute-start.13
  80.6 1.4 collective-permute-start.15
  82.0 98.8 %attn_fwd.1 = (bf16[9,64,1536]{2,1,0:T(8,128)(2,1)}, bf16[9,64,1536]{2,1,0:T(8,128)(2,1)}, bf16[9,1536,128]{2,1,0:T(8,128)(2,1)}, bf16[9,1536,1536]{2,1,0:T(8,12...) custom-call(s32[1,4]{1,0:T(1,128)} %meta.23, ...), custom_call_target="tpu_custom_call" | custom-call | flops 1 | bytes 1 | tf_op jit(solution)/shard_map/attn_fwd/pallas_call | solution.py:176
  181.5 1.8 collective-permute-done.17.refs_5_
  183.4 1.3 collective-permute-done.18.refs_6_
  184.6 1.3 collective-permute-done.19.refs_7_
  186.9 52.3 %ffn.1 = (bf16[1536,768]{1,0:T(8,128)(2,1)}, bf16[1536,3072]{1,0:T(8,128)(2,1)}, bf16[1536,3072]{1,0:T(8,128)(2,1)}, bf16[768,1536]{1,0:T(8,128)(2,1)}, bf16[768...) custom-call(s32[1,4]{1,0:T(1,128)} %meta.23, ...), custom_call_target="tpu_custom_call" | custom-call | flops 1 | bytes 1 | tf_op jit(solution)/shard_map/ffn/pallas_call | solution.py:286
  239.2 15.8 %wgrad_u.1 = (bf16[2,2,4,96,960]{4,3,2,1,0:T(8,128)(2,1)S(1)}, bf16[2,2,4,96,960]{4,3,2,1,0:T(8,128)(2,1)S(1)}) custom-call(s32[1,4]{1,0:T(1,128)S(1)} %copy-done.10, bf16[768,1536]{1,0:T(8,128)(2,1)} %get-tuple-element.176.hid_t, bf16[1536,3072]{1,0:T(8,128)(2,1)} %get-tuple-element.177.gu, bf16[768,1536]{1,0:T(8,128)(2,1)} %get-tuple-element.178.gol_t, ...), custom_call_target="tpu_custom_call" | custom-call | flops 1 | bytes 1 | tf_op jit(solution)/shard_map/wgrad_u/pallas_call | solution.py:404
  256.1 11.3 %wgrad_d.1 = (bf16[2,2,4,104,768]{4,3,2,1,0:T(8,128)(2,1)S(1)}, bf16[2,2,4,104,768]{4,3,2,1,0:T(8,128)(2,1)S(1)}) custom-call(s32[1,4]{1,0:T(1,128)S(1)} %copy-done.10, bf16[768,1536]{1,0:T(8,128)(2,1)} %get-tuple-element.182.gl_t, bf16[1536,3072]{1,0:T(8,128)(2,1)} %get-tuple-element.183.act, f32[4,8,768]{2,1,0:T(8,128)} %maximum_maximum_fusion.vecs), custom_call_target="tpu_custom_call" | custom-call | flops 1 | bytes 1 | tf_op jit(solution)/shard_map/wgrad_d/pallas_call | solution.py:404
  267.9 2.5 fusion
  270.4 1.7 collective-permute-start.22
  272.4 1.6 fusion.2
  274.2 1.8 collective-permute-start.23
  276.0 28.5 %attn_bwd.3 = (bf16[2,3,3,64,1536]{4,3,2,1,0:T(8,128)(2,1)}, f32[6,3,64]{2,1,0:T(4,128)}) custom-call(s32[1,4]{1,0:T(1,128)} %meta.23, bf16[9,1536,1536]{2,1,0:T(8,128)(2,1)} %get-tuple-element.195.e, bf16[9,1536,128]{2,1,0:T(8,128)(2,1)} %get-tuple-element.196.v_d, bf16[12,64,1536]{2,1,0:T(8,128)(2,1)} %get-tuple-element.223.do_t, ...), custom_call_target="tpu_custom_call" | custom-call | flops 1 | bytes 1 | tf_op jit(solution)/shard_map/attn_bwd/pallas_call | solution.py:340
  305.8 1.7 collective-permute-done.22
  307.5 2.5 fusion.3
  310.1 2.7 fusion.1
  312.8 7.4 %wgrad_q.2 = (bf16[2,2,2,104,576]{4,3,2,1,0:T(8,128)(2,1)}, bf16[2,2,2,104,576]{4,3,2,1,0:T(8,128)(2,1)S(1)}) custom-call(s32[1,4]{1,0:T(1,128)S(1)} %copy-done.11, bf16[768,1536]{1,0:T(8,128)(2,1)} %get-tuple-element.162.refs_8_.tok_t, bf16[2,576,1536]{2,1,0:T(8,128)(2,1)} %bitcast.185, f32[2,1,576]{2,1,0:T(1,128)} %reshape.340.refs_1_), custom_call_target="tpu_custom_call" | custom-call | flops 1 | bytes 1 | tf_op jit(solution)/shard_map/wgrad_q/pallas_call | solution.py:404
  321.2 1.4 collective-permute-start.24
  323.3 16.3 %attn_bwd.4 = (bf16[1,3,3,64,1536]{4,3,2,1,0:T(8,128)(2,1)}, f32[3,3,64]{2,1,0:T(4,128)}) custom-call(s32[1,4]{1,0:T(1,128)} %meta.23, bf16[3,1536,1536]{2,1,0:T(8,128)(2,1)} %get-tuple-element.209.e, bf16[3,1536,128]{2,1,0:T(8,128)(2,1)} %get-tuple-element.210.v_d, bf16[12,64,1536]{2,1,0:T(8,128)(2,1)} %get-tuple-element.223.do_t, ...), custom_call_target="tpu_custom_call" | custom-call | flops 1 | bytes 1 | tf_op jit(solution)/shard_map/attn_bwd/pallas_call | solution.py:340
  339.7 1.8 collective-permute-done.24
  341.4 2.1 fusion.22
  343.5 2.4 fusion.14
  345.9 1.2 fusion.8
  347.1 1.5 collective-permute-start.29
  349.4 3.0 collective-permute-start.28
  353.9 16.3 %attn_bwd.5 = (bf16[1,3,3,64,1536]{4,3,2,1,0:T(8,128)(2,1)}, f32[3,3,64]{2,1,0:T(4,128)}) custom-call(s32[1,4]{1,0:T(1,128)} %meta.23, bf16[9,1536,1536]{2,1,0:T(8,128)(2,1)} %get-tuple-element.195.e, bf16[9,1536,128]{2,1,0:T(8,128)(2,1)} %get-tuple-element.196.v_d, bf16[12,64,1536]{2,1,0:T(8,128)(2,1)} %get-tuple-element.223.do_t, ...), custom_call_target="tpu_custom_call" | custom-call | flops 1 | bytes 1 | tf_op jit(solution)/shard_map/attn_bwd/pallas_call | solution.py:340
  370.2 1.1 fusion.9
  371.3 1.3 collective-permute-start.32
  375.0 7.4 %wgrad_q.3 = (bf16[2,2,2,104,576]{4,3,2,1,0:T(8,128)(2,1)S(1)}, bf16[2,2,2,104,576]{4,3,2,1,0:T(8,128)(2,1)S(1)}) custom-call(s32[1,4]{1,0:T(1,128)S(1)} %copy-done.12, bf16[768,1536]{1,0:T(8,128)(2,1)} %get-tuple-element.162.refs_8_.tok_t, bf16[1,576,1536]{2,1,0:T(8,128)(2,1)} %bitcast.188, bf16[1,576,1536]{2,1,0:T(8,128)(2,1)} %bitcast.191, ...), custom_call_target="tpu_custom_call" | custom-call | flops 1 | bytes 1 | tf_op jit(solution)/shard_map/wgrad_q/pallas_call | solution.py:404
  382.5 7.8 %collective-permute-done.32 = bf16[104,1728]{1,0:T(8,128)(2,1)} collective-permute-done((bf16[104,1728]{1,0:T(8,128)(2,1)}, bf16[104,1728]{1,0:T(8,128)(2,1)}, u32[]{:S(2)}, u32[]{:S(2)}) %collective-permute-start.32) | collective-permute-done | bytes 359456 | tf_op jit(solution)/shard_map/ppermute | solution.py:475
  390.3 1.2 fusion.32
  391.7 3.4 collective-permute-start.34
  395.1 1.4 add_convert_fusion.3
  397.4 1.7 collective-permute-start.39
  399.2 2.3 copy-done.2
  401.5 1.5 copy-done.4
  403.0 4.2 input_grad.2.refs_6_
  407.8 1.1 collective-permute-start.36
  408.9 2.1 collective-permute-start.37
  411.0 7.0 %input_grad.3 = f32[1536,768]{1,0:T(8,128)} custom-call(bf16[1,576,1536]{2,1,0:T(8,128)(2,1)S(1)} %bitcast.190, bf16[2,576,1536]{2,1,0:T(8,128)(2,1)S(1)} %bitcast.187, bf16[1,576,1536]{2,1,0:T(8,128)(2,1)S(1)} %bitcast.193, bf16[1,768,768]{2,1,0:T(8,128)(2,1)S(1)} %copy-done.5, bf16[3,768,768]{2,1,0:T(8,128)(2,1)S(1)} %copy-done, ...), custom_call_target="tpu_custom_call", output_to_operand_aliasing={{}: (6, {})} | custom-call | flops 1 | bytes 1 | tf_op jit(solution)/shard_map/input_grad/pallas_call | solution.py:460
  418.0 3.6 collective-permute-done.37
  422.0 1.1 collective-permute-start.41
  423.5 4.9 %collective-permute-done.40 = bf16[104,576]{1,0:T(8,128)(2,1)S(1)} collective-permute-done((bf16[104,576]{1,0:T(8,128)(2,1)S(1)}, bf16[104,576]{1,0:T(8,128)(2,1)S(1)}, u32[]{:S(2)}, u32[]{:S(2)}) %collective-permute-start.40) | collective-permute-done | bytes 119840 | tf_op jit(solution)/shard_map/ppermute | solution.py:475
  428.8 1.0 collective-permute-start.43
  429.8 1.7 collective-permute-start.44
  432.4 2.8 collective-permute-done.43
  435.2 3.1 collective-permute-done.44
  439.5 5.1 %final_du.1 = (f32[768,768]{1,0:T(8,128)}, f32[768,768]{1,0:T(8,128)}, f32[192,768]{1,0:T(8,128)}, f32[8,768]{1,0:T(8,128)}) custom-call(s32[1,4]{1,0:T(1,128)} %meta.23, bf16[4,104,1728]{2,1,0:T(8,128)(2,1)} %copy-done.13, bf16[4,104,1728]{2,1,0:T(8,128)(2,1)} %copy-done.19), custom_call_target="tpu_custom_call" | custom-call | flops 1 | bytes 1 | tf_op jit(solution)/shard_map/final_du/pallas_call | solution.py:435
  444.5 1.7 slice_reduce_fusion
  447.1 3.1 final_q.1
  (212 shorter events, 26.0 us)
Async XLA Ops:
  2.8 49.2 %collective-permute-start = (bf16[104,768]{1,0:T(8,128)(2,1)S(1)}, bf16[104,768]{1,0:T(8,128)(2,1)S(1)}, u32[]{:S(2)}, u32[]{:S(2)}) collective-permute-start(bf16[104,768]{1,0:T(8,128)(2,1)S(1)} %fusion.34), channel_id=1, source_target_pairs={{1,0},{2,1},{3,2},{0,3},{5,4},{6,5},{7,6},{4,7},{9,8},{10,9},{11,1... | collective-permute-start | bytes 479240 | tf_op jit(solution)/shard_map/ppermute | solution.py:470
  7.9 44.1 %collective-permute-start.1 = (bf16[104,768]{1,0:T(8,128)(2,1)S(1)}, bf16[104,768]{1,0:T(8,128)(2,1)S(1)}, u32[]{:S(2)}, u32[]{:S(2)}) collective-permute-start(bf16[104,768]{1,0:T(8,128)(2,1)S(1)} %fusion.34), channel_id=1, source_target_pairs={{2,0},{3,1},{0,2},{1,3},{6,4},{7,5},{4,6},{5,7},{10,8},{11,9},{8,1... | collective-permute-start | bytes 479240 | tf_op jit(solution)/shard_map/ppermute | solution.py:470
  7.9 44.1 %collective-permute-start.2 = (bf16[104,768]{1,0:T(8,128)(2,1)S(1)}, bf16[104,768]{1,0:T(8,128)(2,1)S(1)}, u32[]{:S(2)}, u32[]{:S(2)}) collective-permute-start(bf16[104,768]{1,0:T(8,128)(2,1)S(1)} %fusion.34), channel_id=1, source_target_pairs={{3,0},{0,1},{1,2},{2,3},{7,4},{4,5},{5,6},{6,7},{11,8},{8,9},{9,10... | collective-permute-start | bytes 479240 | tf_op jit(solution)/shard_map/ppermute | solution.py:470
  9.9 42.1 %collective-permute-start.3 = (bf16[96,1536]{1,0:T(8,128)(2,1)S(1)}, bf16[96,1536]{1,0:T(8,128)(2,1)S(1)}, u32[]{:S(2)}, u32[]{:S(2)}) collective-permute-start(bf16[96,1536]{1,0:T(8,128)(2,1)S(1)} %pad_maximum_fusion.4), channel_id=1, source_target_pairs={{1,0},{2,1},{3,2},{0,3},{5,4},{6,5},{7,6},{4,7},{9,8},{10,9},{11,1... | collective-permute-start | bytes 884744 | tf_op jit(solution)/shard_map/ppermute | solution.py:470
  15.0 36.2 %copy-start.39 = (bf16[768]{0:T(1024)(128)(2,1)S(1)}, bf16[768]{0:T(1024)(128)(2,1)}, u32[]{:S(2)}) copy-start(bf16[768]{0:T(1024)(128)(2,1)} %param.21) | copy-start | bytes 4612
  15.0 36.2 %copy-start.40 = (bf16[768]{0:T(1024)(128)(2,1)S(1)}, bf16[768]{0:T(1024)(128)(2,1)}, u32[]{:S(2)}) copy-start(bf16[768]{0:T(1024)(128)(2,1)} %param.22) | copy-start | bytes 4612
  15.0 36.3 %copy-start.41 = (bf16[768]{0:T(1024)(128)(2,1)S(1)}, bf16[768]{0:T(1024)(128)(2,1)}, u32[]{:S(2)}) copy-start(bf16[768]{0:T(1024)(128)(2,1)} %param.26) | copy-start | bytes 4612
  15.0 36.3 %copy-start.42 = (bf16[768]{0:T(1024)(128)(2,1)S(1)}, bf16[768]{0:T(1024)(128)(2,1)}, u32[]{:S(2)}) copy-start(bf16[768]{0:T(1024)(128)(2,1)} %param.27) | copy-start | bytes 4612
  15.0 36.3 %copy-start.43 = (bf16[768]{0:T(1024)(128)(2,1)S(1)}, bf16[768]{0:T(1024)(128)(2,1)}, u32[]{:S(2)}) copy-start(bf16[768]{0:T(1024)(128)(2,1)} %param.28) | copy-start | bytes 4612
  15.0 36.3 %copy-start.44 = (bf16[768]{0:T(1024)(128)(2,1)S(1)}, bf16[768]{0:T(1024)(128)(2,1)}, u32[]{:S(2)}) copy-start(bf16[768]{0:T(1024)(128)(2,1)} %param.20) | copy-start | bytes 4612
  52.0 20.6 %collective-permute-start.8 = (bf16[96,1536]{1,0:T(8,128)(2,1)S(1)}, bf16[96,1536]{1,0:T(8,128)(2,1)S(1)}, u32[]{:S(2)}, u32[]{:S(2)}) collective-permute-start(bf16[96,1536]{1,0:T(8,128)(2,1)S(1)} %pad_maximum_fusion.4), channel_id=1, source_target_pairs={{2,0},{3,1},{0,2},{1,3},{6,4},{7,5},{4,6},{5,7},{10,8},{11,9},{8,1... | collective-permute-start | bytes 884744 | tf_op jit(solution)/shard_map/ppermute | solution.py:470
  53.2 19.5 %collective-permute-start.9 = (bf16[96,1536]{1,0:T(8,128)(2,1)S(1)}, bf16[96,1536]{1,0:T(8,128)(2,1)S(1)}, u32[]{:S(2)}, u32[]{:S(2)}) collective-permute-start(bf16[96,1536]{1,0:T(8,128)(2,1)S(1)} %pad_maximum_fusion.4), channel_id=1, source_target_pairs={{3,0},{0,1},{1,2},{2,3},{7,4},{4,5},{5,6},{6,7},{11,8},{8,9},{9,10... | collective-permute-start | bytes 884744 | tf_op jit(solution)/shard_map/ppermute | solution.py:470
  53.4 28.7 %copy-start.18 = (bf16[3,96,768]{2,1,0:T(8,128)(2,1)}, bf16[3,96,768]{2,1,0:T(8,128)(2,1)S(1)}, u32[]{:S(2)}) copy-start(bf16[3,96,768]{2,1,0:T(8,128)(2,1)S(1)} %pad_maximum_fusion.3.refs_0_) | copy-start | bytes 1327108
  53.4 19.3 %collective-permute-start.5 = (bf16[3,96,768]{2,1,0:T(8,128)(2,1)S(1)}, bf16[3,96,768]{2,1,0:T(8,128)(2,1)S(1)}, u32[]{:S(2)}, u32[]{:S(2)}) collective-permute-start(bf16[3,96,768]{2,1,0:T(8,128)(2,1)S(1)} %pad_maximum_fusion.3.refs_0_), channel_id=1, source_target_pairs={{0,8},{4,12},{8,0},{12,4},{16,24},{20,28},{24,16},{28,20},{1,9},{5... | collective-permute-start | bytes 1327112 | tf_op jit(solution)/shard_map/ppermute | solution.py:479
  54.9 19.5 %collective-permute-start.6 = (bf16[3,96,768]{2,1,0:T(8,128)(2,1)S(1)}, bf16[3,96,768]{2,1,0:T(8,128)(2,1)S(1)}, u32[]{:S(2)}, u32[]{:S(2)}) collective-permute-start(bf16[3,96,768]{2,1,0:T(8,128)(2,1)S(1)} %pad_maximum_fusion.3.refs_0_), channel_id=1, source_target_pairs={{0,16},{4,20},{8,24},{12,28},{16,0},{20,4},{24,8},{28,12},{1,17},{... | collective-permute-start | bytes 1327112 | tf_op jit(solution)/shard_map/ppermute | solution.py:479
  56.4 18.0 %collective-permute-start.7 = (bf16[3,96,768]{2,1,0:T(8,128)(2,1)S(1)}, bf16[3,96,768]{2,1,0:T(8,128)(2,1)S(1)}, u32[]{:S(2)}, u32[]{:S(2)}) collective-permute-start(bf16[3,96,768]{2,1,0:T(8,128)(2,1)S(1)} %pad_maximum_fusion.3.refs_0_), channel_id=1, source_target_pairs={{0,24},{4,28},{8,16},{12,20},{16,8},{20,12},{24,0},{28,4},{1,25},{... | collective-permute-start | bytes 1327112 | tf_op jit(solution)/shard_map/ppermute | solution.py:479
  72.7 2.4 collective-permute-start.4
  74.4 1.9 collective-permute-start.10
  74.5 2.4 collective-permute-start.11
  75.0 2.5 collective-permute-start.12
  78.4 102.4 %copy-start.14 = (bf16[3,96,1536]{2,1,0:T(8,128)(2,1)}, bf16[3,96,1536]{2,1,0:T(8,128)(2,1)S(1)}, u32[]{:S(2)}) copy-start(bf16[3,96,1536]{2,1,0:T(8,128)(2,1)S(1)} %pad_maximum_fusion.1.refs_0_) | copy-start | bytes 2654212
  78.5 102.4 %collective-permute-start.13 = (bf16[3,96,1536]{2,1,0:T(8,128)(2,1)S(1)}, bf16[3,96,1536]{2,1,0:T(8,128)(2,1)S(1)}, u32[]{:S(2)}, u32[]{:S(2)}) collective-permute-start(bf16[3,96,1536]{2,1,0:T(8,128)(2,1)S(1)} %pad_maximum_fusion.1.refs_0_), channel_id=1, source_target_pairs={{0,8},{4,12},{8,0},{12,4},{16,24},{20,28},{24,16},{28,20},{1,9},{5... | collective-permute-start | bytes 2654216 | tf_op jit(solution)/shard_map/ppermute | solution.py:479
  79.9 100.9 %collective-permute-start.14 = (bf16[3,96,1536]{2,1,0:T(8,128)(2,1)S(1)}, bf16[3,96,1536]{2,1,0:T(8,128)(2,1)S(1)}, u32[]{:S(2)}, u32[]{:S(2)}) collective-permute-start(bf16[3,96,1536]{2,1,0:T(8,128)(2,1)S(1)} %pad_maximum_fusion.1.refs_0_), channel_id=1, source_target_pairs={{0,16},{4,20},{8,24},{12,28},{16,0},{20,4},{24,8},{28,12},{1,17},{... | collective-permute-start | bytes 2654216 | tf_op jit(solution)/shard_map/ppermute | solution.py:479
  80.6 100.2 %collective-permute-start.15 = (bf16[3,96,1536]{2,1,0:T(8,128)(2,1)S(1)}, bf16[3,96,1536]{2,1,0:T(8,128)(2,1)S(1)}, u32[]{:S(2)}, u32[]{:S(2)}) collective-permute-start(bf16[3,96,1536]{2,1,0:T(8,128)(2,1)S(1)} %pad_maximum_fusion.1.refs_0_), channel_id=1, source_target_pairs={{0,24},{4,28},{8,16},{12,20},{16,8},{20,12},{24,0},{28,4},{1,25},{... | collective-permute-start | bytes 2654216 | tf_op jit(solution)/shard_map/ppermute | solution.py:479
  82.0 98.9 %collective-permute-start.16 = (bf16[3,96,1536]{2,1,0:T(8,128)(2,1)S(1)}, bf16[3,96,1536]{2,1,0:T(8,128)(2,1)}, u32[]{:S(2)}, u32[]{:S(2)}) collective-permute-start(bf16[3,96,1536]{2,1,0:T(8,128)(2,1)S(1)} %pad_maximum_fusion.1.refs_0_), channel_id=1, source_target_pairs={{0,4},{4,0},{8,12},{12,8},{16,20},{20,16},{24,28},{28,24},{1,5},{5... | collective-permute-start | bytes 2654216 | tf_op jit(solution)/shard_map/ppermute | solution.py:479
  180.9 2.5 collective-permute-start.17
  181.0 3.7 collective-permute-start.18
  181.5 4.4 collective-permute-start.19
  186.8 52.4 %copy-start.10 = (s32[1,4]{1,0:T(1,128)S(1)}, s32[1,4]{1,0:T(1,128)}, u32[]{:S(2)}) copy-start(s32[1,4]{1,0:T(1,128)} %meta.23) | copy-start | bytes 52
  239.2 16.1 %copy-start.35 = (f32[8,768]{1,0:T(8,128)S(1)}, f32[8,768]{1,0:T(8,128)}, u32[]{:S(2)}) copy-start(f32[8,768]{1,0:T(8,128)} %get-tuple-element.184) | copy-start | bytes 73732
  255.1 12.4 %collective-permute-start.20 = (bf16[2,2,4,96,960]{4,3,2,1,0:T(8,128)(2,1)S(1)}, bf16[2,2,4,96,960]{4,3,2,1,0:T(8,128)(2,1)S(1)}, u32[]{:S(2)}, u32[]{:S(2)}) collective-permute-start(bf16[2,2,4,96,960]{4,3,2,1,0:T(8,128)(2,1)S(1)} %get-tuple-element.179), channel_id=1, source_target_pairs={{0,4},{4,0},{8,12},{12,8},{16,20},{20,16},{24,28},{28,24},{1,5},{5... | collective-permute-start | bytes 8847368 | tf_op jit(solution)/shard_map/ppermute | solution.py:479
  267.5 4.9 %collective-permute-start.21 = (bf16[2,2,4,104,768]{4,3,2,1,0:T(8,128)(2,1)S(1)}, bf16[2,2,4,104,768]{4,3,2,1,0:T(8,128)(2,1)S(1)}, u32[]{:S(2)}, u32[]{:S(2)}) collective-permute-start(bf16[2,2,4,104,768]{4,3,2,1,0:T(8,128)(2,1)S(1)} %get-tuple-element.187), channel_id=1, source_target_pairs={{0,4},{4,0},{8,12},{12,8},{16,20},{20,16},{24,28},{28,24},{1,5},{5... | collective-permute-start | bytes 7667720 | tf_op jit(solution)/shard_map/ppermute | solution.py:479
  270.4 37.1 %collective-permute-start.22 = (bf16[2,4,96,960]{3,2,1,0:T(8,128)(2,1)}, bf16[2,4,96,960]{3,2,1,0:T(8,128)(2,1)}, u32[]{:S(2)}, u32[]{:S(2)}) collective-permute-start(bf16[2,4,96,960]{3,2,1,0:T(8,128)(2,1)} %fusion), channel_id=1, source_target_pairs={{0,16},{4,20},{8,24},{12,28},{16,0},{20,4},{24,8},{28,12},{1,17},{... | collective-permute-start | bytes 4423688 | tf_op jit(solution)/shard_map/ppermute | solution.py:479
  274.2 33.3 %collective-permute-start.23 = (bf16[2,4,104,768]{3,2,1,0:T(8,128)(2,1)}, bf16[2,4,104,768]{3,2,1,0:T(8,128)(2,1)}, u32[]{:S(2)}, u32[]{:S(2)}) collective-permute-start(bf16[2,4,104,768]{3,2,1,0:T(8,128)(2,1)} %fusion.2), channel_id=1, source_target_pairs={{0,8},{4,12},{8,0},{12,4},{16,24},{20,28},{24,16},{28,20},{1,9},{5... | collective-permute-start | bytes 3833864 | tf_op jit(solution)/shard_map/ppermute | solution.py:479
  321.2 20.3 %collective-permute-start.26 = (bf16[2,2,2,104,576]{4,3,2,1,0:T(8,128)(2,1)}, bf16[2,2,2,104,576]{4,3,2,1,0:T(8,128)(2,1)}, u32[]{:S(2)}, u32[]{:S(2)}) collective-permute-start(bf16[2,2,2,104,576]{4,3,2,1,0:T(8,128)(2,1)} %get-tuple-element.208), channel_id=1, source_target_pairs={{0,4},{4,0},{8,12},{12,8},{16,20},{20,16},{24,28},{28,24},{1,5},{5... | collective-permute-start | bytes 2875400 | tf_op jit(solution)/shard_map/ppermute | solution.py:479
  321.2 20.3 %collective-permute-start.24 = (bf16[4,96,960]{2,1,0:T(8,128)(2,1)}, bf16[4,96,960]{2,1,0:T(8,128)(2,1)}, u32[]{:S(2)}, u32[]{:S(2)}) collective-permute-start(bf16[4,96,960]{2,1,0:T(8,128)(2,1)} %fusion.1), channel_id=1, source_target_pairs={{0,8},{4,12},{8,0},{12,4},{16,24},{20,28},{24,16},{28,20},{1,9},{5... | collective-permute-start | bytes 2211848 | tf_op jit(solution)/shard_map/ppermute | solution.py:479
  322.6 17.1 %collective-permute-start.25 = (bf16[4,104,768]{2,1,0:T(8,128)(2,1)}, bf16[4,104,768]{2,1,0:T(8,128)(2,1)}, u32[]{:S(2)}, u32[]{:S(2)}) collective-permute-start(bf16[4,104,768]{2,1,0:T(8,128)(2,1)} %fusion.3), channel_id=1, source_target_pairs={{0,16},{4,20},{8,24},{12,28},{16,0},{20,4},{24,8},{28,12},{1,17},{... | collective-permute-start | bytes 1916936 | tf_op jit(solution)/shard_map/ppermute | solution.py:479
  347.1 23.1 %collective-permute-start.29 = (bf16[2,2,104,576]{3,2,1,0:T(8,128)(2,1)S(1)}, bf16[2,2,104,576]{3,2,1,0:T(8,128)(2,1)S(1)}, u32[]{:S(2)}, u32[]{:S(2)}) collective-permute-start(bf16[2,2,104,576]{3,2,1,0:T(8,128)(2,1)S(1)} %fusion.8), channel_id=1, source_target_pairs={{0,8},{4,12},{8,0},{12,4},{16,24},{20,28},{24,16},{28,20},{1,9},{5... | collective-permute-start | bytes 1437704 | tf_op jit(solution)/shard_map/ppermute | solution.py:479
  349.4 20.8 %collective-permute-start.28 = (bf16[104,1728]{1,0:T(8,128)(2,1)}, bf16[104,1728]{1,0:T(8,128)(2,1)}, u32[]{:S(2)}, u32[]{:S(2)}) collective-permute-start(bf16[104,1728]{1,0:T(8,128)(2,1)} %fusion.18), channel_id=1, source_target_pairs={{0,3},{1,0},{2,1},{3,2},{4,7},{5,4},{6,5},{7,6},{8,11},{9,8},{10,9... | collective-permute-start | bytes 1078280 | tf_op jit(solution)/shard_map/ppermute | solution.py:475
  353.1 17.1 %collective-permute-start.27 = (bf16[104,1728]{1,0:T(8,128)(2,1)}, bf16[104,1728]{1,0:T(8,128)(2,1)}, u32[]{:S(2)}, u32[]{:S(2)}) collective-permute-start(bf16[104,1728]{1,0:T(8,128)(2,1)} %fusion.17), channel_id=1, source_target_pairs={{0,1},{1,2},{2,3},{3,0},{4,5},{5,6},{6,7},{7,4},{8,9},{9,10},{10,1... | collective-permute-start | bytes 1078280 | tf_op jit(solution)/shard_map/ppermute | solution.py:475
  353.9 16.3 %copy-start.9 = (bf16[2,2,2,104,576]{4,3,2,1,0:T(8,128)(2,1)S(1)}, bf16[2,2,2,104,576]{4,3,2,1,0:T(8,128)(2,1)}, u32[]{:S(2)}) copy-start(bf16[2,2,2,104,576]{4,3,2,1,0:T(8,128)(2,1)} %copy-done.7) | copy-start | bytes 2875396
  353.9 18.7 %copy-start.38 = (f32[3,3,64]{2,1,0:T(4,128)S(1)}, f32[3,3,64]{2,1,0:T(4,128)}, u32[]{:S(2)}) copy-start(f32[3,3,64]{2,1,0:T(4,128)} %get-tuple-element.229) | copy-start | bytes 6916
  353.9 21.1 %copy-start.12 = (s32[1,4]{1,0:T(1,128)S(1)}, s32[1,4]{1,0:T(1,128)}, u32[]{:S(2)}) copy-start(s32[1,4]{1,0:T(1,128)} %meta.23) | copy-start | bytes 52
  353.9 45.2 %copy-start.5 = (bf16[1,768,768]{2,1,0:T(8,128)(2,1)S(1)}, bf16[1,768,768]{2,1,0:T(8,128)(2,1)}, u32[]{:S(2)}) copy-start(bf16[1,768,768]{2,1,0:T(8,128)(2,1)} %get-tuple-element.171.refs_12_.refs_3_) | copy-start | bytes 3538948
  371.3 19.0 %collective-permute-start.32 = (bf16[104,1728]{1,0:T(8,128)(2,1)}, bf16[104,1728]{1,0:T(8,128)(2,1)}, u32[]{:S(2)}, u32[]{:S(2)}) collective-permute-start(bf16[104,1728]{1,0:T(8,128)(2,1)} %fusion.20), channel_id=1, source_target_pairs={{0,2},{1,3},{2,0},{3,1},{4,6},{5,7},{6,4},{7,5},{8,10},{9,11},{10,... | collective-permute-start | bytes 1078280 | tf_op jit(solution)/shard_map/ppermute | solution.py:475
  373.5 9.0 %collective-permute-start.31 = (bf16[2,104,576]{2,1,0:T(8,128)(2,1)S(1)}, bf16[2,104,576]{2,1,0:T(8,128)(2,1)S(1)}, u32[]{:S(2)}, u32[]{:S(2)}) collective-permute-start(bf16[2,104,576]{2,1,0:T(8,128)(2,1)S(1)} %fusion.9), channel_id=1, source_target_pairs={{0,16},{4,20},{8,24},{12,28},{16,0},{20,4},{24,8},{28,12},{1,17},{... | collective-permute-start | bytes 718856 | tf_op jit(solution)/shard_map/ppermute | solution.py:479
  375.0 24.2 %copy-start = (bf16[3,768,768]{2,1,0:T(8,128)(2,1)S(1)}, bf16[3,768,768]{2,1,0:T(8,128)(2,1)}, u32[]{:S(2)}) copy-start(bf16[3,768,768]{2,1,0:T(8,128)(2,1)} %get-tuple-element.172.refs_13_.refs_4_) | copy-start | bytes 10616836
  375.0 24.2 %copy-start.1 = (bf16[2,3,3,64,1536]{4,3,2,1,0:T(8,128)(2,1)S(1)}, bf16[2,3,3,64,1536]{4,3,2,1,0:T(8,128)(2,1)}, u32[]{:S(2)}) copy-start(bf16[2,3,3,64,1536]{4,3,2,1,0:T(8,128)(2,1)} %get-tuple-element.202) | copy-start | bytes 10616836
  382.4 24.8 %collective-permute-start.30 = (bf16[2,2,2,104,576]{4,3,2,1,0:T(8,128)(2,1)S(1)}, bf16[2,2,2,104,576]{4,3,2,1,0:T(8,128)(2,1)S(1)}, u32[]{:S(2)}, u32[]{:S(2)}) collective-permute-start(bf16[2,2,2,104,576]{4,3,2,1,0:T(8,128)(2,1)S(1)} %get-tuple-element.231), channel_id=1, source_target_pairs={{0,4},{4,0},{8,12},{12,8},{16,20},{20,16},{24,28},{28,24},{1,5},{5... | collective-permute-start | bytes 2875400 | tf_op jit(solution)/shard_map/ppermute | solution.py:479
  391.6 15.6 %collective-permute-start.33 = (bf16[104,576]{1,0:T(8,128)(2,1)S(1)}, bf16[104,576]{1,0:T(8,128)(2,1)S(1)}, u32[]{:S(2)}, u32[]{:S(2)}) collective-permute-start(bf16[104,576]{1,0:T(8,128)(2,1)S(1)} %get-tuple-element.288), channel_id=1, source_target_pairs={{0,1},{1,2},{2,3},{3,0},{4,5},{5,6},{6,7},{7,4},{8,9},{9,10},{10,1... | collective-permute-start | bytes 359432 | tf_op jit(solution)/shard_map/ppermute | solution.py:475
  391.7 15.5 %collective-permute-start.34 = (bf16[104,576]{1,0:T(8,128)(2,1)S(1)}, bf16[104,576]{1,0:T(8,128)(2,1)S(1)}, u32[]{:S(2)}, u32[]{:S(2)}) collective-permute-start(bf16[104,576]{1,0:T(8,128)(2,1)S(1)} %get-tuple-element.287), channel_id=1, source_target_pairs={{0,2},{1,3},{2,0},{3,1},{4,6},{5,7},{6,4},{7,5},{8,10},{9,11},{10,... | collective-permute-start | bytes 359432 | tf_op jit(solution)/shard_map/ppermute | solution.py:475
  396.5 21.5 %collective-permute-start.38 = (bf16[104,1728]{1,0:T(8,128)(2,1)S(1)}, bf16[104,1728]{1,0:T(8,128)(2,1)S(1)}, u32[]{:S(2)}, u32[]{:S(2)}) collective-permute-start(bf16[104,1728]{1,0:T(8,128)(2,1)S(1)} %add_convert_fusion.3), channel_id=1, source_target_pairs={{0,8},{4,12},{8,0},{12,4},{16,24},{20,28},{24,16},{28,20},{1,9},{5... | collective-permute-start | bytes 1078280 | tf_op jit(solution)/shard_map/ppermute | solution.py:479
  397.4 20.5 %collective-permute-start.39 = (bf16[104,1728]{1,0:T(8,128)(2,1)S(1)}, bf16[104,1728]{1,0:T(8,128)(2,1)S(1)}, u32[]{:S(2)}, u32[]{:S(2)}) collective-permute-start(bf16[104,1728]{1,0:T(8,128)(2,1)S(1)} %add_convert_fusion.3), channel_id=1, source_target_pairs={{0,16},{4,20},{8,24},{12,28},{16,0},{20,4},{24,8},{28,12},{1,17},{... | collective-permute-start | bytes 1078280 | tf_op jit(solution)/shard_map/ppermute | solution.py:479
  407.4 10.6 %collective-permute-start.35 = (bf16[2,104,576]{2,1,0:T(8,128)(2,1)S(1)}, bf16[2,104,576]{2,1,0:T(8,128)(2,1)S(1)}, u32[]{:S(2)}, u32[]{:S(2)}) collective-permute-start(bf16[2,104,576]{2,1,0:T(8,128)(2,1)S(1)} %get-tuple-element.291), channel_id=1, source_target_pairs={{0,16},{4,20},{8,24},{12,28},{16,0},{20,4},{24,8},{28,12},{1,17},{... | collective-permute-start | bytes 718856 | tf_op jit(solution)/shard_map/ppermute | solution.py:479
  407.8 10.2 %collective-permute-start.36 = (bf16[2,104,576]{2,1,0:T(8,128)(2,1)S(1)}, bf16[2,104,576]{2,1,0:T(8,128)(2,1)S(1)}, u32[]{:S(2)}, u32[]{:S(2)}) collective-permute-start(bf16[2,104,576]{2,1,0:T(8,128)(2,1)S(1)} %get-tuple-element.290), channel_id=1, source_target_pairs={{0,8},{4,12},{8,0},{12,4},{16,24},{20,28},{24,16},{28,20},{1,9},{5... | collective-permute-start | bytes 718856 | tf_op jit(solution)/shard_map/ppermute | solution.py:479
  408.9 12.7 %collective-permute-start.37 = (bf16[2,104,576]{2,1,0:T(8,128)(2,1)S(1)}, bf16[2,104,576]{2,1,0:T(8,128)(2,1)S(1)}, u32[]{:S(2)}, u32[]{:S(2)}) collective-permute-start(bf16[2,104,576]{2,1,0:T(8,128)(2,1)S(1)} %get-tuple-element.289), channel_id=1, source_target_pairs={{0,24},{4,28},{8,16},{12,20},{16,8},{20,12},{24,0},{28,4},{1,25},{... | collective-permute-start | bytes 718856 | tf_op jit(solution)/shard_map/ppermute | solution.py:479
  421.6 6.8 %collective-permute-start.42 = (bf16[56,1728]{1,0:T(8,128)(2,1)S(1)}, bf16[56,1728]{1,0:T(8,128)(2,1)S(1)}, u32[]{:S(2)}, u32[]{:S(2)}) collective-permute-start(bf16[56,1728]{1,0:T(8,128)(2,1)S(1)} %slice.423), channel_id=1, source_target_pairs={{0,16},{4,20},{8,24},{12,28},{16,0},{20,4},{24,8},{28,12},{1,17},{... | collective-permute-start | bytes 580616 | tf_op jit(solution)/shard_map/ppermute | solution.py:479
  422.0 6.4 %collective-permute-start.41 = (bf16[48,1728]{1,0:T(8,128)(2,1)S(1)}, bf16[48,1728]{1,0:T(8,128)(2,1)S(1)}, u32[]{:S(2)}, u32[]{:S(2)}) collective-permute-start(bf16[48,1728]{1,0:T(8,128)(2,1)S(1)} %slice.422), channel_id=1, source_target_pairs={{0,8},{4,12},{8,0},{12,4},{16,24},{20,28},{24,16},{28,20},{1,9},{5... | collective-permute-start | bytes 497672 | tf_op jit(solution)/shard_map/ppermute | solution.py:479
  423.4 5.0 %collective-permute-start.40 = (bf16[104,576]{1,0:T(8,128)(2,1)S(1)}, bf16[104,576]{1,0:T(8,128)(2,1)S(1)}, u32[]{:S(2)}, u32[]{:S(2)}) collective-permute-start(bf16[104,576]{1,0:T(8,128)(2,1)S(1)} %slice_bitcast_fusion.3), channel_id=1, source_target_pairs={{0,3},{1,0},{2,1},{3,2},{4,7},{5,4},{6,5},{7,6},{8,11},{9,8},{10,9... | collective-permute-start | bytes 359432 | tf_op jit(solution)/shard_map/ppermute | solution.py:475
  428.7 9.7 %collective-permute-start.46 = (bf16[4,104,1728]{2,1,0:T(8,128)(2,1)S(1)}, bf16[4,104,1728]{2,1,0:T(8,128)(2,1)S(1)}, u32[]{:S(2)}, u32[]{:S(2)}) collective-permute-start(bf16[4,104,1728]{2,1,0:T(8,128)(2,1)S(1)} %pad_maximum_fusion.x), channel_id=1, source_target_pairs={{0,4},{4,0},{8,12},{12,8},{16,20},{20,16},{24,28},{28,24},{1,5},{5... | collective-permute-start | bytes 4313096 | tf_op jit(solution)/shard_map/ppermute | solution.py:479
  428.8 6.4 %collective-permute-start.43 = (bf16[104,576]{1,0:T(8,128)(2,1)S(1)}, bf16[104,576]{1,0:T(8,128)(2,1)S(1)}, u32[]{:S(2)}, u32[]{:S(2)}) collective-permute-start(bf16[104,576]{1,0:T(8,128)(2,1)S(1)} %fusion.31), channel_id=1, source_target_pairs={{0,8},{4,12},{8,0},{12,4},{16,24},{20,28},{24,16},{28,20},{1,9},{5... | collective-permute-start | bytes 359432 | tf_op jit(solution)/shard_map/ppermute | solution.py:479
  429.8 8.5 %collective-permute-start.44 = (bf16[104,576]{1,0:T(8,128)(2,1)S(1)}, bf16[104,576]{1,0:T(8,128)(2,1)S(1)}, u32[]{:S(2)}, u32[]{:S(2)}) collective-permute-start(bf16[104,576]{1,0:T(8,128)(2,1)S(1)} %fusion.31), channel_id=1, source_target_pairs={{0,16},{4,20},{8,24},{12,28},{16,0},{20,4},{24,8},{28,12},{1,17},{... | collective-permute-start | bytes 359432 | tf_op jit(solution)/shard_map/ppermute | solution.py:479
  431.5 6.8 %collective-permute-start.45 = (bf16[104,576]{1,0:T(8,128)(2,1)S(1)}, bf16[104,576]{1,0:T(8,128)(2,1)S(1)}, u32[]{:S(2)}, u32[]{:S(2)}) collective-permute-start(bf16[104,576]{1,0:T(8,128)(2,1)S(1)} %fusion.31), channel_id=1, source_target_pairs={{0,24},{4,28},{8,16},{12,20},{16,8},{20,12},{24,0},{28,4},{1,25},{... | collective-permute-start | bytes 359432 | tf_op jit(solution)/shard_map/ppermute | solution.py:479
  438.5 7.8 %collective-permute-start.47 = (bf16[4,104,576]{2,1,0:T(8,128)(2,1)S(1)}, bf16[4,104,576]{2,1,0:T(8,128)(2,1)S(1)}, u32[]{:S(2)}, u32[]{:S(2)}) collective-permute-start(bf16[4,104,576]{2,1,0:T(8,128)(2,1)S(1)} %pad_maximum_fusion.2.x), channel_id=1, source_target_pairs={{0,4},{4,0},{8,12},{12,8},{16,20},{20,16},{24,28},{28,24},{1,5},{5... | collective-permute-start | bytes 1437704 | tf_op jit(solution)/shard_map/ppermute | solution.py:479
  (30 other events, 115.6 us)
where the time goes:
time: 460 us; the launch traced here: 452 us
  Pallas kernels  310 us (67%)
  waiting for transfers between devices  48.9 us (11%)
  starting transfers between devices  46.7 us (10%)
  other arithmetic  27 us (6%)
  local copies, waits for them, and re-layouts  17.9 us (4%)
    pallas_call x2, Pallas kernels, attn_fwd(): pl.pallas_call(functools.partial(attn_fwd_kernel, C=C, KC=min(128, C), G=...  135 us
    pallas_call x3, Pallas kernels, attn_bwd(): pl.pallas_call(functools.partial(attn_bwd_kernel, C=C, KC=min(256, C)), g...  61.1 us
    pallas_call x1, Pallas kernels, ffn(): pl.pallas_call(functools.partial(ffn_kernel, R=R, layout=layout), grid=(C...  52.3 us
    pallas_call x4, Pallas kernels, wgrad(): pl.pallas_call(kernel, grid=(J,), in_specs=[SMEM] + specs, out_specs=[spe...  42 us
    ppermute x36, starting transfers between devices, flip(): lax.ppermute(x, 'wide', [(i, i ^ bit) for i in range(lax.axis_size('wide'...  28.6 us
    ppermute x36, waiting for transfers between devices, flip(): lax.ppermute(x, 'wide', [(i, i ^ bit) for i in range(lax.axis_size('wide'...  21.8 us
    convert_element_type x13, other arithmetic, total(): return x.astype(bf)  19.2 us
    ppermute x6, waiting for transfers between devices, fetch(): return lax.ppermute(x, 'narrow', [((i + s) % n, i) for i in range(n)])  14.3 us
  transfers between devices with their start and end apart: 48, of which 16 were waited for; matrix products, arithmetic and copies ran while one was open for 5% of the time, Pallas kernels for 51%

commit v1 on v0

--- a/solution.py
+++ b/solution.py
@@ -58,7 +58,7 @@
 
 def attn_fwd_kernel(meta, *refs, C, KC, G, layout, own):
     pieces, refs = refs[:len(layout)], refs[len(layout):]
-    x, b, cos, sin, q_t, k_t, v_d, e, ctx, linv, w_t, *rest = refs
+    x, b, cos, sin, q_t, k_t, v_d, e, ctx, exact, linv, w_t, *rest = refs
     if own:
         x_t, Q2, KD, VA, S, W, flag, sem = rest
     else:
@@ -155,7 +155,9 @@
     o = dg(VA[...], e[...], 1, 0)
     inv = 1.0 / o[HD:HD + 1]
     linv[...] = inv
-    ctx[...] = (o[:HD] * inv).astype(bf)
+    o = o[:HD] * inv
+    exact[...] = o
+    ctx[...] = o.astype(bf)
 
 
 def attn_fwd(meta, pieces, layout, x, b, cos, sin, own):
@@ -166,10 +168,10 @@
     at = lambda h: (h, 0, 0)
     fix = lambda a: pl.BlockSpec(a.shape, lambda h: (0,) * a.ndim, pipeline_mode=pl.Buffered(1))
     hb = pl.BlockSpec((None, HD, C), at)
-    out_specs = [hb, hb, pl.BlockSpec((None, C, 2 * HD), at), pl.BlockSpec((None, C, C), at), hb,
+    out_specs = [hb, hb, pl.BlockSpec((None, C, 2 * HD), at), pl.BlockSpec((None, C, C), at), hb, hb,
                  pl.BlockSpec((None, 1, C), at), pl.BlockSpec((None, D, D), lambda h: (h // G, 0, 0))]
     out_shape = [shape((H, HD, C), bf), shape((H, HD, C), bf), shape((H, C, 2 * HD), bf), shape((H, C, C), bf),
-                 shape((H, HD, C), bf), shape((H, 1, C), f32), shape((groups, D, D), bf)]
+                 shape((H, HD, C), bf), shape((H, HD, C), f32), shape((H, 1, C), f32), shape((groups, D, D), bf)]
     if own:
         out_specs.append(pl.BlockSpec((D, C), lambda h: (0, 0)))
         out_shape.append(shape((D, C), bf))
@@ -299,7 +301,7 @@
     length = length_of(meta)
     g = do_t[...].astype(f32)
     inv = linv[...]
-    DI[...] = jnp.sum(g * ctx[...].astype(f32), axis=0, keepdims=True) * inv
+    DI[...] = jnp.sum(g * ctx[...], axis=0, keepdims=True) * inv
     g = g * inv
     hi = g.astype(bf)
     D2[:HD, :] = hi
@@ -535,7 +537,7 @@
     b_own = qkv_bias.astype(f32).reshape(1, 3, G, HD).transpose(0, 2, 1, 3)
     ud_piece = jnp.concatenate([cut(up_weight), cut(down_weight)], axis=1)
     ud_got = [fetch(tie(ud_piece, q_piece), 1)]
-    q0, k0, v0, e0, c0, l0, wt0, tok_t = attn_fwd(meta, [qkv_t, out_weight], (0, 1), tok, b_own, cos, sin, True)
+    q0, k0, v0, e0, c0, o0, l0, wt0, tok_t = attn_fwd(meta, [qkv_t, out_weight], (0, 1), tok, b_own, cos, sin, True)
     got, ud_got, tok_t = lax.optimization_barrier((got, ud_got, tok_t))
     biases = jnp.stack([bias] + [x[rows:rows + 2] for x in got]).reshape(J, 2 * D).astype(f32)
     bq, ub = biases[1:, :N].reshape(J - 1, 3, G, HD).transpose(0, 2, 1, 3), biases[:, N:N + F]
@@ -552,7 +554,7 @@
     ud_near = [flip(ud, rel) for rel in NEAR[1:]]
     ud_far = [flip(ud, 1)]
     tok_t = tie(tok_t, ud)
-    q1, k1, v1, e1, c1, l1, wt1 = attn_fwd(meta, q_pieces, q_places, tok_t, bq, cos, sin, False)
+    q1, k1, v1, e1, c1, o1, l1, wt1 = attn_fwd(meta, q_pieces, q_places, tok_t, bq, cos, sin, False)
     ud_near, ud_far, c1 = lax.optimization_barrier((ud_near, ud_far, c1))
     ud_pieces = [ud] + ud_near + ud_far + [flip(x, 1) for x in ud_near]
     ud_places = [(rel | low, 0, rows) for low in (0, 1) for rel in NEAR]
@@ -582,7 +584,7 @@
             n, rows + EXTRA, N, [(SPLIT, rows, N)], "wgrad_q", 2 * C * D * n * N)
 
     def backward(group, count, do_t):
-        saved, shift = ((e0, v0, c0, l0, q0, k0), 0) if group == 0 else ((e1, v1, c1, l1, q1, k1), G)
+        saved, shift = ((e0, v0, o0, l0, q0, k0), 0) if group == 0 else ((e1, v1, o1, l1, q1, k1), G)
         gp, gb = attn_bwd(meta, saved, do_t, cos, sin, G, group * G - shift, shift, count * G)
         return gp.reshape(count, N, C), gb.reshape(count, G, 3, HD).transpose(0, 2, 1, 3).reshape(count, 1, N)
 

time: 460 us -> 459 us (level)
  transfers between devices with their start and end apart: 48 -> 48, of which waited for: 16 -> 17; matrix products, arithmetic and copies ran while one was open for 5% -> 4% of each run, Pallas kernels for 51% -> 51%
where the time goes in v1:
time: 459 us; the launch traced here: 452 us
  Pallas kernels  310 us (68%)
  waiting for transfers between devices  50.8 us (11%)
  starting transfers between devices  44.3 us (10%)
  other arithmetic  26.8 us (6%)
  local copies, waits for them, and re-layouts  17.9 us (4%)
    pallas_call x2, Pallas kernels, attn_fwd(): pl.pallas_call(functools.partial(attn_fwd_kernel, C=C, KC=min(128, C), G=...  135 us
    pallas_call x3, Pallas kernels, attn_bwd(): pl.pallas_call(functools.partial(attn_bwd_kernel, C=C, KC=min(256, C)), g...  61.7 us
    pallas_call x1, Pallas kernels, ffn(): pl.pallas_call(functools.partial(ffn_kernel, R=R, layout=layout), grid=(C...  52.4 us
    pallas_call x4, Pallas kernels, wgrad(): pl.pallas_call(kernel, grid=(J,), in_specs=[SMEM] + specs, out_specs=[spe...  42 us
    ppermute x36, starting transfers between devices, flip(): lax.ppermute(x, 'wide', [(i, i ^ bit) for i in range(lax.axis_size('wide'...  28.2 us
    ppermute x36, waiting for transfers between devices, flip(): lax.ppermute(x, 'wide', [(i, i ^ bit) for i in range(lax.axis_size('wide'...  24.4 us
    convert_element_type x13, other arithmetic, total(): return x.astype(bf)  19 us
    ppermute x6, waiting for transfers between devices, fetch(): return lax.ppermute(x, 'narrow', [((i + s) % n, i) for i in range(n)])  13.5 us
  transfers between devices with their start and end apart: 48, of which 17 were waited for; matrix products, arithmetic and copies ran while one was open for 4% of the time, Pallas kernels for 51%

profile of v1, /device:TPU:0, one launch (start us, length us, event | category | flops | bytes accessed | tf_op | source)
XLA Modules:
  0.0 452.1 jit_solution(16309687092233511052)
XLA Ops:
  0.7 1.6 copy.37
  2.8 5.1 %collective-permute-start = (bf16[104,768]{1,0:T(8,128)(2,1)S(1)}, bf16[104,768]{1,0:T(8,128)(2,1)S(1)}, u32[]{:S(2)}, u32[]{:S(2)}) collective-permute-start(bf16[104,768]{1,0:T(8,128)(2,1)S(1)} %fusion.34), channel_id=1, source_target_pairs={{1,0},{2,1},{3,2},{0,3},{5,4},{6,5},{7,6},{4,7},{9,8},{10,9},{11,1... | collective-permute-start | bytes 479240 | tf_op jit(solution)/shard_map/ppermute | solution.py:472
  7.9 1.0 collective-permute-start.2
  8.9 1.0 constant_dynamic-slice_fusion
  9.9 2.9 collective-permute-start.3
  12.8 1.5 multiply_sine_fusion
  15.0 36.2 %attn_fwd_own.1 = (bf16[3,64,1536]{2,1,0:T(8,128)(2,1)}, bf16[3,64,1536]{2,1,0:T(8,128)(2,1)}, bf16[3,1536,128]{2,1,0:T(8,128)(2,1)}, bf16[3,1536,1536]{2,1,0:T(...) custom-call(s32[1,4]{1,0:T(1,128)} %meta.23, ...), custom_call_target="tpu_custom_call" | custom-call | flops 1 | bytes 1 | tf_op jit(solution)/shard_map/attn_fwd_own/pallas_call | solution.py:178
  52.4 2.6 collective-permute-start.5
  55.5 1.1 collective-permute-start.7
  58.0 13.5 %collective-permute-done.8 = bf16[96,1536]{1,0:T(8,128)(2,1)S(1)} collective-permute-done((bf16[96,1536]{1,0:T(8,128)(2,1)S(1)}, bf16[96,1536]{1,0:T(8,128)(2,1)S(1)}, u32[]{:S(2)}, u32[]{:S(2)}) %collective-permute-start.8) | collective-permute-done | bytes 294944 | tf_op jit(solution)/shard_map/ppermute | solution.py:472
  71.5 3.1 collective-permute-done.6.refs_2_
  75.3 1.2 collective-permute-done.10.refs_5_
  79.5 1.0 collective-permute-start.14
  80.4 1.8 collective-permute-start.15
  82.3 98.8 %attn_fwd.1 = (bf16[9,64,1536]{2,1,0:T(8,128)(2,1)}, bf16[9,64,1536]{2,1,0:T(8,128)(2,1)}, bf16[9,1536,128]{2,1,0:T(8,128)(2,1)}, bf16[9,1536,1536]{2,1,0:T(8,12...) custom-call(s32[1,4]{1,0:T(1,128)} %meta.23, ...), custom_call_target="tpu_custom_call" | custom-call | flops 1 | bytes 1 | tf_op jit(solution)/shard_map/attn_fwd/pallas_call | solution.py:178
  181.8 1.8 collective-permute-done.17.refs_5_
  183.7 1.3 collective-permute-done.18.refs_6_
  184.9 1.3 collective-permute-done.19.refs_7_
  187.2 52.4 %ffn.1 = (bf16[1536,768]{1,0:T(8,128)(2,1)}, bf16[1536,3072]{1,0:T(8,128)(2,1)}, bf16[1536,3072]{1,0:T(8,128)(2,1)}, bf16[768,1536]{1,0:T(8,128)(2,1)}, bf16[768...) custom-call(s32[1,4]{1,0:T(1,128)} %meta.23, ...), custom_call_target="tpu_custom_call" | custom-call | flops 1 | bytes 1 | tf_op jit(solution)/shard_map/ffn/pallas_call | solution.py:288
  239.6 15.8 %wgrad_u.1 = (bf16[2,2,4,96,960]{4,3,2,1,0:T(8,128)(2,1)S(1)}, bf16[2,2,4,96,960]{4,3,2,1,0:T(8,128)(2,1)S(1)}) custom-call(s32[1,4]{1,0:T(1,128)S(1)} %copy-done.10, bf16[768,1536]{1,0:T(8,128)(2,1)} %get-tuple-element.178.hid_t, bf16[1536,3072]{1,0:T(8,128)(2,1)} %get-tuple-element.179.gu, bf16[768,1536]{1,0:T(8,128)(2,1)} %get-tuple-element.180.gol_t, ...), custom_call_target="tpu_custom_call" | custom-call | flops 1 | bytes 1 | tf_op jit(solution)/shard_map/wgrad_u/pallas_call | solution.py:406
  256.4 11.3 %wgrad_d.1 = (bf16[2,2,4,104,768]{4,3,2,1,0:T(8,128)(2,1)S(1)}, bf16[2,2,4,104,768]{4,3,2,1,0:T(8,128)(2,1)S(1)}) custom-call(s32[1,4]{1,0:T(1,128)S(1)} %copy-done.10, bf16[768,1536]{1,0:T(8,128)(2,1)} %get-tuple-element.184.gl_t, bf16[1536,3072]{1,0:T(8,128)(2,1)} %get-tuple-element.185.act, f32[4,8,768]{2,1,0:T(8,128)} %maximum_maximum_fusion.vecs), custom_call_target="tpu_custom_call" | custom-call | flops 1 | bytes 1 | tf_op jit(solution)/shard_map/wgrad_d/pallas_call | solution.py:406
  268.2 2.3 fusion
  270.5 1.2 collective-permute-start.22
  272.7 1.6 fusion.2
  274.6 1.1 collective-permute-start.23
  275.6 28.8 %attn_bwd.3 = (bf16[2,3,3,64,1536]{4,3,2,1,0:T(8,128)(2,1)}, f32[6,3,64]{2,1,0:T(4,128)}) custom-call(s32[1,4]{1,0:T(1,128)} %meta.23, bf16[9,1536,1536]{2,1,0:T(8,128)(2,1)} %get-tuple-element.197.e, bf16[9,1536,128]{2,1,0:T(8,128)(2,1)} %get-tuple-element.198.v_d, bf16[12,64,1536]{2,1,0:T(8,128)(2,1)} %get-tuple-element.227.do_t, ...), custom_call_target="tpu_custom_call" | custom-call | flops 1 | bytes 1 | tf_op jit(solution)/shard_map/attn_bwd/pallas_call | solution.py:342
  305.8 1.5 collective-permute-done.22
  307.3 2.5 fusion.3
  309.8 2.7 fusion.1
  312.5 7.4 %wgrad_q.2 = (bf16[2,2,2,104,576]{4,3,2,1,0:T(8,128)(2,1)}, bf16[2,2,2,104,576]{4,3,2,1,0:T(8,128)(2,1)S(1)}) custom-call(s32[1,4]{1,0:T(1,128)S(1)} %copy-done.11, bf16[768,1536]{1,0:T(8,128)(2,1)} %get-tuple-element.164.refs_8_.tok_t, bf16[2,576,1536]{2,1,0:T(8,128)(2,1)} %bitcast.185, f32[2,1,576]{2,1,0:T(1,128)} %reshape.340.refs_1_), custom_call_target="tpu_custom_call" | custom-call | flops 1 | bytes 1 | tf_op jit(solution)/shard_map/wgrad_q/pallas_call | solution.py:406
  319.9 1.0 copy-done.7
  321.0 1.1 collective-permute-start.24
  322.1 1.0 collective-permute-start.25
  323.1 16.5 %attn_bwd.4 = (bf16[1,3,3,64,1536]{4,3,2,1,0:T(8,128)(2,1)}, f32[3,3,64]{2,1,0:T(4,128)}) custom-call(s32[1,4]{1,0:T(1,128)} %meta.23, bf16[3,1536,1536]{2,1,0:T(8,128)(2,1)} %get-tuple-element.212.e, bf16[3,1536,128]{2,1,0:T(8,128)(2,1)} %get-tuple-element.213.v_d, bf16[12,64,1536]{2,1,0:T(8,128)(2,1)} %get-tuple-element.227.do_t, ...), custom_call_target="tpu_custom_call" | custom-call | flops 1 | bytes 1 | tf_op jit(solution)/shard_map/attn_bwd/pallas_call | solution.py:342
  339.6 1.6 collective-permute-done.24
  341.2 2.1 fusion.22
  343.3 2.4 fusion.14
  345.7 1.2 fusion.8
  346.9 1.2 collective-permute-start.29
  348.9 3.5 collective-permute-start.28
  354.0 16.4 %attn_bwd.5 = (bf16[1,3,3,64,1536]{4,3,2,1,0:T(8,128)(2,1)}, f32[3,3,64]{2,1,0:T(4,128)}) custom-call(s32[1,4]{1,0:T(1,128)} %meta.23, bf16[9,1536,1536]{2,1,0:T(8,128)(2,1)} %get-tuple-element.197.e, bf16[9,1536,128]{2,1,0:T(8,128)(2,1)} %get-tuple-element.198.v_d, bf16[12,64,1536]{2,1,0:T(8,128)(2,1)} %get-tuple-element.227.do_t, ...), custom_call_target="tpu_custom_call" | custom-call | flops 1 | bytes 1 | tf_op jit(solution)/shard_map/attn_bwd/pallas_call | solution.py:342
  370.4 1.1 fusion.9
  374.5 7.4 %wgrad_q.3 = (bf16[2,2,2,104,576]{4,3,2,1,0:T(8,128)(2,1)S(1)}, bf16[2,2,2,104,576]{4,3,2,1,0:T(8,128)(2,1)S(1)}) custom-call(s32[1,4]{1,0:T(1,128)S(1)} %copy-done.12, bf16[768,1536]{1,0:T(8,128)(2,1)} %get-tuple-element.164.refs_8_.tok_t, bf16[1,576,1536]{2,1,0:T(8,128)(2,1)} %bitcast.188, bf16[1,576,1536]{2,1,0:T(8,128)(2,1)} %bitcast.191, ...), custom_call_target="tpu_custom_call" | custom-call | flops 1 | bytes 1 | tf_op jit(solution)/shard_map/wgrad_q/pallas_call | solution.py:406
  382.0 8.5 %collective-permute-done.32 = bf16[104,1728]{1,0:T(8,128)(2,1)} collective-permute-done((bf16[104,1728]{1,0:T(8,128)(2,1)}, bf16[104,1728]{1,0:T(8,128)(2,1)}, u32[]{:S(2)}, u32[]{:S(2)}) %collective-permute-start.32) | collective-permute-done | bytes 359456 | tf_op jit(solution)/shard_map/ppermute | solution.py:477
  390.5 1.2 fusion.32
  391.8 2.0 collective-permute-start.34
  393.8 1.4 add_convert_fusion.3
  395.2 2.3 collective-permute-start.38
  397.9 2.3 copy-done.2
  400.3 1.5 copy-done.4
  401.7 4.2 input_grad.2.refs_6_
  406.1 1.7 collective-permute-start.35
  407.9 1.8 collective-permute-start.37
  409.7 7.0 %input_grad.3 = f32[1536,768]{1,0:T(8,128)} custom-call(bf16[1,576,1536]{2,1,0:T(8,128)(2,1)S(1)} %bitcast.190, bf16[2,576,1536]{2,1,0:T(8,128)(2,1)S(1)} %bitcast.187, bf16[1,576,1536]{2,1,0:T(8,128)(2,1)S(1)} %bitcast.193, bf16[1,768,768]{2,1,0:T(8,128)(2,1)S(1)} %copy-done.5, bf16[3,768,768]{2,1,0:T(8,128)(2,1)S(1)} %copy-done, ...), custom_call_target="tpu_custom_call", output_to_operand_aliasing={{}: (6, {})} | custom-call | flops 1 | bytes 1 | tf_op jit(solution)/shard_map/input_grad/pallas_call | solution.py:462
  417.2 3.1 collective-permute-done.37
  420.3 1.7 collective-permute-start.42
  423.3 4.4 collective-permute-done.40
  428.1 1.7 collective-permute-start.43
  430.2 1.4 collective-permute-start.45
  431.7 2.7 collective-permute-done.43
  434.3 4.0 collective-permute-done.44
  439.5 5.1 %final_du.1 = (f32[768,768]{1,0:T(8,128)}, f32[768,768]{1,0:T(8,128)}, f32[192,768]{1,0:T(8,128)}, f32[8,768]{1,0:T(8,128)}) custom-call(s32[1,4]{1,0:T(1,128)} %meta.23, bf16[4,104,1728]{2,1,0:T(8,128)(2,1)} %copy-done.13, bf16[4,104,1728]{2,1,0:T(8,128)(2,1)} %copy-done.19), custom_call_target="tpu_custom_call" | custom-call | flops 1 | bytes 1 | tf_op jit(solution)/shard_map/final_du/pallas_call | solution.py:437
  444.5 1.7 slice_reduce_fusion
  447.1 3.1 final_q.1
  (212 shorter events, 25.5 us)
Async XLA Ops:
  2.8 49.3 %collective-permute-start = (bf16[104,768]{1,0:T(8,128)(2,1)S(1)}, bf16[104,768]{1,0:T(8,128)(2,1)S(1)}, u32[]{:S(2)}, u32[]{:S(2)}) collective-permute-start(bf16[104,768]{1,0:T(8,128)(2,1)S(1)} %fusion.34), channel_id=1, source_target_pairs={{1,0},{2,1},{3,2},{0,3},{5,4},{6,5},{7,6},{4,7},{9,8},{10,9},{11,1... | collective-permute-start | bytes 479240 | tf_op jit(solution)/shard_map/ppermute | solution.py:472
  7.9 44.2 %collective-permute-start.1 = (bf16[104,768]{1,0:T(8,128)(2,1)S(1)}, bf16[104,768]{1,0:T(8,128)(2,1)S(1)}, u32[]{:S(2)}, u32[]{:S(2)}) collective-permute-start(bf16[104,768]{1,0:T(8,128)(2,1)S(1)} %fusion.34), channel_id=1, source_target_pairs={{2,0},{3,1},{0,2},{1,3},{6,4},{7,5},{4,6},{5,7},{10,8},{11,9},{8,1... | collective-permute-start | bytes 479240 | tf_op jit(solution)/shard_map/ppermute | solution.py:472
  7.9 44.2 %collective-permute-start.2 = (bf16[104,768]{1,0:T(8,128)(2,1)S(1)}, bf16[104,768]{1,0:T(8,128)(2,1)S(1)}, u32[]{:S(2)}, u32[]{:S(2)}) collective-permute-start(bf16[104,768]{1,0:T(8,128)(2,1)S(1)} %fusion.34), channel_id=1, source_target_pairs={{3,0},{0,1},{1,2},{2,3},{7,4},{4,5},{5,6},{6,7},{11,8},{8,9},{9,10... | collective-permute-start | bytes 479240 | tf_op jit(solution)/shard_map/ppermute | solution.py:472
  9.9 42.2 %collective-permute-start.3 = (bf16[96,1536]{1,0:T(8,128)(2,1)S(1)}, bf16[96,1536]{1,0:T(8,128)(2,1)S(1)}, u32[]{:S(2)}, u32[]{:S(2)}) collective-permute-start(bf16[96,1536]{1,0:T(8,128)(2,1)S(1)} %pad_maximum_fusion.4), channel_id=1, source_target_pairs={{1,0},{2,1},{3,2},{0,3},{5,4},{6,5},{7,6},{4,7},{9,8},{10,9},{11,1... | collective-permute-start | bytes 884744 | tf_op jit(solution)/shard_map/ppermute | solution.py:472
  15.0 36.3 %copy-start.39 = (bf16[768]{0:T(1024)(128)(2,1)S(1)}, bf16[768]{0:T(1024)(128)(2,1)}, u32[]{:S(2)}) copy-start(bf16[768]{0:T(1024)(128)(2,1)} %param.21) | copy-start | bytes 4612
  15.0 36.3 %copy-start.40 = (bf16[768]{0:T(1024)(128)(2,1)S(1)}, bf16[768]{0:T(1024)(128)(2,1)}, u32[]{:S(2)}) copy-start(bf16[768]{0:T(1024)(128)(2,1)} %param.22) | copy-start | bytes 4612
  15.0 36.3 %copy-start.41 = (bf16[768]{0:T(1024)(128)(2,1)S(1)}, bf16[768]{0:T(1024)(128)(2,1)}, u32[]{:S(2)}) copy-start(bf16[768]{0:T(1024)(128)(2,1)} %param.26) | copy-start | bytes 4612
  15.0 36.3 %copy-start.42 = (bf16[768]{0:T(1024)(128)(2,1)S(1)}, bf16[768]{0:T(1024)(128)(2,1)}, u32[]{:S(2)}) copy-start(bf16[768]{0:T(1024)(128)(2,1)} %param.27) | copy-start | bytes 4612
  15.0 36.4 %copy-start.43 = (bf16[768]{0:T(1024)(128)(2,1)S(1)}, bf16[768]{0:T(1024)(128)(2,1)}, u32[]{:S(2)}) copy-start(bf16[768]{0:T(1024)(128)(2,1)} %param.28) | copy-start | bytes 4612
  15.0 36.4 %copy-start.44 = (bf16[768]{0:T(1024)(128)(2,1)S(1)}, bf16[768]{0:T(1024)(128)(2,1)}, u32[]{:S(2)}) copy-start(bf16[768]{0:T(1024)(128)(2,1)} %param.20) | copy-start | bytes 4612
  52.1 19.4 %collective-permute-start.8 = (bf16[96,1536]{1,0:T(8,128)(2,1)S(1)}, bf16[96,1536]{1,0:T(8,128)(2,1)S(1)}, u32[]{:S(2)}, u32[]{:S(2)}) collective-permute-start(bf16[96,1536]{1,0:T(8,128)(2,1)S(1)} %pad_maximum_fusion.4), channel_id=1, source_target_pairs={{2,0},{3,1},{0,2},{1,3},{6,4},{7,5},{4,6},{5,7},{10,8},{11,9},{8,1... | collective-permute-start | bytes 884744 | tf_op jit(solution)/shard_map/ppermute | solution.py:472
  52.2 19.4 %collective-permute-start.9 = (bf16[96,1536]{1,0:T(8,128)(2,1)S(1)}, bf16[96,1536]{1,0:T(8,128)(2,1)S(1)}, u32[]{:S(2)}, u32[]{:S(2)}) collective-permute-start(bf16[96,1536]{1,0:T(8,128)(2,1)S(1)} %pad_maximum_fusion.4), channel_id=1, source_target_pairs={{3,0},{0,1},{1,2},{2,3},{7,4},{4,5},{5,6},{6,7},{11,8},{8,9},{9,10... | collective-permute-start | bytes 884744 | tf_op jit(solution)/shard_map/ppermute | solution.py:472
  52.4 29.9 %copy-start.18 = (bf16[3,96,768]{2,1,0:T(8,128)(2,1)}, bf16[3,96,768]{2,1,0:T(8,128)(2,1)S(1)}, u32[]{:S(2)}) copy-start(bf16[3,96,768]{2,1,0:T(8,128)(2,1)S(1)} %pad_maximum_fusion.3.refs_0_) | copy-start | bytes 1327108
  52.4 19.2 %collective-permute-start.5 = (bf16[3,96,768]{2,1,0:T(8,128)(2,1)S(1)}, bf16[3,96,768]{2,1,0:T(8,128)(2,1)S(1)}, u32[]{:S(2)}, u32[]{:S(2)}) collective-permute-start(bf16[3,96,768]{2,1,0:T(8,128)(2,1)S(1)} %pad_maximum_fusion.3.refs_0_), channel_id=1, source_target_pairs={{0,8},{4,12},{8,0},{12,4},{16,24},{20,28},{24,16},{28,20},{1,9},{5... | collective-permute-start | bytes 1327112 | tf_op jit(solution)/shard_map/ppermute | solution.py:481
  55.0 19.7 %collective-permute-start.6 = (bf16[3,96,768]{2,1,0:T(8,128)(2,1)S(1)}, bf16[3,96,768]{2,1,0:T(8,128)(2,1)S(1)}, u32[]{:S(2)}, u32[]{:S(2)}) collective-permute-start(bf16[3,96,768]{2,1,0:T(8,128)(2,1)S(1)} %pad_maximum_fusion.3.refs_0_), channel_id=1, source_target_pairs={{0,16},{4,20},{8,24},{12,28},{16,0},{20,4},{24,8},{28,12},{1,17},{... | collective-permute-start | bytes 1327112 | tf_op jit(solution)/shard_map/ppermute | solution.py:481
  55.5 19.2 %collective-permute-start.7 = (bf16[3,96,768]{2,1,0:T(8,128)(2,1)S(1)}, bf16[3,96,768]{2,1,0:T(8,128)(2,1)S(1)}, u32[]{:S(2)}, u32[]{:S(2)}) collective-permute-start(bf16[3,96,768]{2,1,0:T(8,128)(2,1)S(1)} %pad_maximum_fusion.3.refs_0_), channel_id=1, source_target_pairs={{0,24},{4,28},{8,16},{12,20},{16,8},{20,12},{24,0},{28,4},{1,25},{... | collective-permute-start | bytes 1327112 | tf_op jit(solution)/shard_map/ppermute | solution.py:481
  71.5 3.8 collective-permute-start.4
  74.7 1.9 collective-permute-start.10
  74.8 2.4 collective-permute-start.11
  75.3 2.5 collective-permute-start.12
  78.7 102.4 %copy-start.14 = (bf16[3,96,1536]{2,1,0:T(8,128)(2,1)}, bf16[3,96,1536]{2,1,0:T(8,128)(2,1)S(1)}, u32[]{:S(2)}) copy-start(bf16[3,96,1536]{2,1,0:T(8,128)(2,1)S(1)} %pad_maximum_fusion.1.refs_0_) | copy-start | bytes 2654212
  78.7 102.4 %collective-permute-start.13 = (bf16[3,96,1536]{2,1,0:T(8,128)(2,1)S(1)}, bf16[3,96,1536]{2,1,0:T(8,128)(2,1)S(1)}, u32[]{:S(2)}, u32[]{:S(2)}) collective-permute-start(bf16[3,96,1536]{2,1,0:T(8,128)(2,1)S(1)} %pad_maximum_fusion.1.refs_0_), channel_id=1, source_target_pairs={{0,8},{4,12},{8,0},{12,4},{16,24},{20,28},{24,16},{28,20},{1,9},{5... | collective-permute-start | bytes 2654216 | tf_op jit(solution)/shard_map/ppermute | solution.py:481
  79.5 101.6 %collective-permute-start.14 = (bf16[3,96,1536]{2,1,0:T(8,128)(2,1)S(1)}, bf16[3,96,1536]{2,1,0:T(8,128)(2,1)S(1)}, u32[]{:S(2)}, u32[]{:S(2)}) collective-permute-start(bf16[3,96,1536]{2,1,0:T(8,128)(2,1)S(1)} %pad_maximum_fusion.1.refs_0_), channel_id=1, source_target_pairs={{0,16},{4,20},{8,24},{12,28},{16,0},{20,4},{24,8},{28,12},{1,17},{... | collective-permute-start | bytes 2654216 | tf_op jit(solution)/shard_map/ppermute | solution.py:481
  80.4 100.7 %collective-permute-start.15 = (bf16[3,96,1536]{2,1,0:T(8,128)(2,1)S(1)}, bf16[3,96,1536]{2,1,0:T(8,128)(2,1)S(1)}, u32[]{:S(2)}, u32[]{:S(2)}) collective-permute-start(bf16[3,96,1536]{2,1,0:T(8,128)(2,1)S(1)} %pad_maximum_fusion.1.refs_0_), channel_id=1, source_target_pairs={{0,24},{4,28},{8,16},{12,20},{16,8},{20,12},{24,0},{28,4},{1,25},{... | collective-permute-start | bytes 2654216 | tf_op jit(solution)/shard_map/ppermute | solution.py:481
  82.3 98.9 %collective-permute-start.16 = (bf16[3,96,1536]{2,1,0:T(8,128)(2,1)S(1)}, bf16[3,96,1536]{2,1,0:T(8,128)(2,1)}, u32[]{:S(2)}, u32[]{:S(2)}) collective-permute-start(bf16[3,96,1536]{2,1,0:T(8,128)(2,1)S(1)} %pad_maximum_fusion.1.refs_0_), channel_id=1, source_target_pairs={{0,4},{4,0},{8,12},{12,8},{16,20},{20,16},{24,28},{28,24},{1,5},{5... | collective-permute-start | bytes 2654216 | tf_op jit(solution)/shard_map/ppermute | solution.py:481
  181.2 2.5 collective-permute-start.17
  181.2 3.7 collective-permute-start.18
  181.7 4.4 collective-permute-start.19
  187.1 52.4 %copy-start.10 = (s32[1,4]{1,0:T(1,128)S(1)}, s32[1,4]{1,0:T(1,128)}, u32[]{:S(2)}) copy-start(s32[1,4]{1,0:T(1,128)} %meta.23) | copy-start | bytes 52
  239.6 16.1 %copy-start.35 = (f32[8,768]{1,0:T(8,128)S(1)}, f32[8,768]{1,0:T(8,128)}, u32[]{:S(2)}) copy-start(f32[8,768]{1,0:T(8,128)} %get-tuple-element.186) | copy-start | bytes 73732
  255.4 12.4 %collective-permute-start.20 = (bf16[2,2,4,96,960]{4,3,2,1,0:T(8,128)(2,1)S(1)}, bf16[2,2,4,96,960]{4,3,2,1,0:T(8,128)(2,1)S(1)}, u32[]{:S(2)}, u32[]{:S(2)}) collective-permute-start(bf16[2,2,4,96,960]{4,3,2,1,0:T(8,128)(2,1)S(1)} %get-tuple-element.181), channel_id=1, source_target_pairs={{0,4},{4,0},{8,12},{12,8},{16,20},{20,16},{24,28},{28,24},{1,5},{5... | collective-permute-start | bytes 8847368 | tf_op jit(solution)/shard_map/ppermute | solution.py:481
  267.8 4.9 %collective-permute-start.21 = (bf16[2,2,4,104,768]{4,3,2,1,0:T(8,128)(2,1)S(1)}, bf16[2,2,4,104,768]{4,3,2,1,0:T(8,128)(2,1)S(1)}, u32[]{:S(2)}, u32[]{:S(2)}) collective-permute-start(bf16[2,2,4,104,768]{4,3,2,1,0:T(8,128)(2,1)S(1)} %get-tuple-element.189), channel_id=1, source_target_pairs={{0,4},{4,0},{8,12},{12,8},{16,20},{20,16},{24,28},{28,24},{1,5},{5... | collective-permute-start | bytes 7667720 | tf_op jit(solution)/shard_map/ppermute | solution.py:481
  270.5 36.7 %collective-permute-start.22 = (bf16[2,4,96,960]{3,2,1,0:T(8,128)(2,1)}, bf16[2,4,96,960]{3,2,1,0:T(8,128)(2,1)}, u32[]{:S(2)}, u32[]{:S(2)}) collective-permute-start(bf16[2,4,96,960]{3,2,1,0:T(8,128)(2,1)} %fusion), channel_id=1, source_target_pairs={{0,16},{4,20},{8,24},{12,28},{16,0},{20,4},{24,8},{28,12},{1,17},{... | collective-permute-start | bytes 4423688 | tf_op jit(solution)/shard_map/ppermute | solution.py:481
  274.6 32.7 %collective-permute-start.23 = (bf16[2,4,104,768]{3,2,1,0:T(8,128)(2,1)}, bf16[2,4,104,768]{3,2,1,0:T(8,128)(2,1)}, u32[]{:S(2)}, u32[]{:S(2)}) collective-permute-start(bf16[2,4,104,768]{3,2,1,0:T(8,128)(2,1)} %fusion.2), channel_id=1, source_target_pairs={{0,8},{4,12},{8,0},{12,4},{16,24},{20,28},{24,16},{28,20},{1,9},{5... | collective-permute-start | bytes 3833864 | tf_op jit(solution)/shard_map/ppermute | solution.py:481
  321.0 20.3 %collective-permute-start.26 = (bf16[2,2,2,104,576]{4,3,2,1,0:T(8,128)(2,1)}, bf16[2,2,2,104,576]{4,3,2,1,0:T(8,128)(2,1)}, u32[]{:S(2)}, u32[]{:S(2)}) collective-permute-start(bf16[2,2,2,104,576]{4,3,2,1,0:T(8,128)(2,1)} %get-tuple-element.211), channel_id=1, source_target_pairs={{0,4},{4,0},{8,12},{12,8},{16,20},{20,16},{24,28},{28,24},{1,5},{5... | collective-permute-start | bytes 2875400 | tf_op jit(solution)/shard_map/ppermute | solution.py:481
  321.0 20.3 %collective-permute-start.24 = (bf16[4,96,960]{2,1,0:T(8,128)(2,1)}, bf16[4,96,960]{2,1,0:T(8,128)(2,1)}, u32[]{:S(2)}, u32[]{:S(2)}) collective-permute-start(bf16[4,96,960]{2,1,0:T(8,128)(2,1)} %fusion.1), channel_id=1, source_target_pairs={{0,8},{4,12},{8,0},{12,4},{16,24},{20,28},{24,16},{28,20},{1,9},{5... | collective-permute-start | bytes 2211848 | tf_op jit(solution)/shard_map/ppermute | solution.py:481
  322.1 17.5 %collective-permute-start.25 = (bf16[4,104,768]{2,1,0:T(8,128)(2,1)}, bf16[4,104,768]{2,1,0:T(8,128)(2,1)}, u32[]{:S(2)}, u32[]{:S(2)}) collective-permute-start(bf16[4,104,768]{2,1,0:T(8,128)(2,1)} %fusion.3), channel_id=1, source_target_pairs={{0,16},{4,20},{8,24},{12,28},{16,0},{20,4},{24,8},{28,12},{1,17},{... | collective-permute-start | bytes 1916936 | tf_op jit(solution)/shard_map/ppermute | solution.py:481
  346.9 23.5 %collective-permute-start.29 = (bf16[2,2,104,576]{3,2,1,0:T(8,128)(2,1)S(1)}, bf16[2,2,104,576]{3,2,1,0:T(8,128)(2,1)S(1)}, u32[]{:S(2)}, u32[]{:S(2)}) collective-permute-start(bf16[2,2,104,576]{3,2,1,0:T(8,128)(2,1)S(1)} %fusion.8), channel_id=1, source_target_pairs={{0,8},{4,12},{8,0},{12,4},{16,24},{20,28},{24,16},{28,20},{1,9},{5... | collective-permute-start | bytes 1437704 | tf_op jit(solution)/shard_map/ppermute | solution.py:481
  348.9 21.5 %collective-permute-start.28 = (bf16[104,1728]{1,0:T(8,128)(2,1)}, bf16[104,1728]{1,0:T(8,128)(2,1)}, u32[]{:S(2)}, u32[]{:S(2)}) collective-permute-start(bf16[104,1728]{1,0:T(8,128)(2,1)} %fusion.18), channel_id=1, source_target_pairs={{0,3},{1,0},{2,1},{3,2},{4,7},{5,4},{6,5},{7,6},{8,11},{9,8},{10,9... | collective-permute-start | bytes 1078280 | tf_op jit(solution)/shard_map/ppermute | solution.py:477
  353.2 17.2 %collective-permute-start.27 = (bf16[104,1728]{1,0:T(8,128)(2,1)}, bf16[104,1728]{1,0:T(8,128)(2,1)}, u32[]{:S(2)}, u32[]{:S(2)}) collective-permute-start(bf16[104,1728]{1,0:T(8,128)(2,1)} %fusion.17), channel_id=1, source_target_pairs={{0,1},{1,2},{2,3},{3,0},{4,5},{5,6},{6,7},{7,4},{8,9},{9,10},{10,1... | collective-permute-start | bytes 1078280 | tf_op jit(solution)/shard_map/ppermute | solution.py:477
  353.9 16.5 %copy-start.9 = (bf16[2,2,2,104,576]{4,3,2,1,0:T(8,128)(2,1)S(1)}, bf16[2,2,2,104,576]{4,3,2,1,0:T(8,128)(2,1)}, u32[]{:S(2)}) copy-start(bf16[2,2,2,104,576]{4,3,2,1,0:T(8,128)(2,1)} %copy-done.7) | copy-start | bytes 2875396
  353.9 18.2 %copy-start.38 = (f32[3,3,64]{2,1,0:T(4,128)S(1)}, f32[3,3,64]{2,1,0:T(4,128)}, u32[]{:S(2)}) copy-start(f32[3,3,64]{2,1,0:T(4,128)} %get-tuple-element.233) | copy-start | bytes 6916
  353.9 20.6 %copy-start.12 = (s32[1,4]{1,0:T(1,128)S(1)}, s32[1,4]{1,0:T(1,128)}, u32[]{:S(2)}) copy-start(s32[1,4]{1,0:T(1,128)} %meta.23) | copy-start | bytes 52
  354.0 43.9 %copy-start.5 = (bf16[1,768,768]{2,1,0:T(8,128)(2,1)S(1)}, bf16[1,768,768]{2,1,0:T(8,128)(2,1)}, u32[]{:S(2)}) copy-start(bf16[1,768,768]{2,1,0:T(8,128)(2,1)} %get-tuple-element.173.refs_12_.refs_3_) | copy-start | bytes 3538948
  371.5 19.0 %collective-permute-start.32 = (bf16[104,1728]{1,0:T(8,128)(2,1)}, bf16[104,1728]{1,0:T(8,128)(2,1)}, u32[]{:S(2)}, u32[]{:S(2)}) collective-permute-start(bf16[104,1728]{1,0:T(8,128)(2,1)} %fusion.20), channel_id=1, source_target_pairs={{0,2},{1,3},{2,0},{3,1},{4,6},{5,7},{6,4},{7,5},{8,10},{9,11},{10,... | collective-permute-start | bytes 1078280 | tf_op jit(solution)/shard_map/ppermute | solution.py:477
  373.0 9.0 %collective-permute-start.31 = (bf16[2,104,576]{2,1,0:T(8,128)(2,1)S(1)}, bf16[2,104,576]{2,1,0:T(8,128)(2,1)S(1)}, u32[]{:S(2)}, u32[]{:S(2)}) collective-permute-start(bf16[2,104,576]{2,1,0:T(8,128)(2,1)S(1)} %fusion.9), channel_id=1, source_target_pairs={{0,16},{4,20},{8,24},{12,28},{16,0},{20,4},{24,8},{28,12},{1,17},{... | collective-permute-start | bytes 718856 | tf_op jit(solution)/shard_map/ppermute | solution.py:481
  374.5 23.4 %copy-start = (bf16[3,768,768]{2,1,0:T(8,128)(2,1)S(1)}, bf16[3,768,768]{2,1,0:T(8,128)(2,1)}, u32[]{:S(2)}) copy-start(bf16[3,768,768]{2,1,0:T(8,128)(2,1)} %get-tuple-element.174.refs_13_.refs_4_) | copy-start | bytes 10616836
  374.5 23.4 %copy-start.1 = (bf16[2,3,3,64,1536]{4,3,2,1,0:T(8,128)(2,1)S(1)}, bf16[2,3,3,64,1536]{4,3,2,1,0:T(8,128)(2,1)}, u32[]{:S(2)}) copy-start(bf16[2,3,3,64,1536]{4,3,2,1,0:T(8,128)(2,1)} %get-tuple-element.205) | copy-start | bytes 10616836
  381.9 24.0 %collective-permute-start.30 = (bf16[2,2,2,104,576]{4,3,2,1,0:T(8,128)(2,1)S(1)}, bf16[2,2,2,104,576]{4,3,2,1,0:T(8,128)(2,1)S(1)}, u32[]{:S(2)}, u32[]{:S(2)}) collective-permute-start(bf16[2,2,2,104,576]{4,3,2,1,0:T(8,128)(2,1)S(1)} %get-tuple-element.235), channel_id=1, source_target_pairs={{0,4},{4,0},{8,12},{12,8},{16,20},{20,16},{24,28},{28,24},{1,5},{5... | collective-permute-start | bytes 2875400 | tf_op jit(solution)/shard_map/ppermute | solution.py:481
  391.8 14.2 %collective-permute-start.33 = (bf16[104,576]{1,0:T(8,128)(2,1)S(1)}, bf16[104,576]{1,0:T(8,128)(2,1)S(1)}, u32[]{:S(2)}, u32[]{:S(2)}) collective-permute-start(bf16[104,576]{1,0:T(8,128)(2,1)S(1)} %get-tuple-element.292), channel_id=1, source_target_pairs={{0,1},{1,2},{2,3},{3,0},{4,5},{5,6},{6,7},{7,4},{8,9},{9,10},{10,1... | collective-permute-start | bytes 359432 | tf_op jit(solution)/shard_map/ppermute | solution.py:477
  391.8 14.1 %collective-permute-start.34 = (bf16[104,576]{1,0:T(8,128)(2,1)S(1)}, bf16[104,576]{1,0:T(8,128)(2,1)S(1)}, u32[]{:S(2)}, u32[]{:S(2)}) collective-permute-start(bf16[104,576]{1,0:T(8,128)(2,1)S(1)} %get-tuple-element.291), channel_id=1, source_target_pairs={{0,2},{1,3},{2,0},{3,1},{4,6},{5,7},{6,4},{7,5},{8,10},{9,11},{10,... | collective-permute-start | bytes 359432 | tf_op jit(solution)/shard_map/ppermute | solution.py:477
  395.2 21.5 %collective-permute-start.38 = (bf16[104,1728]{1,0:T(8,128)(2,1)S(1)}, bf16[104,1728]{1,0:T(8,128)(2,1)S(1)}, u32[]{:S(2)}, u32[]{:S(2)}) collective-permute-start(bf16[104,1728]{1,0:T(8,128)(2,1)S(1)} %add_convert_fusion.3), channel_id=1, source_target_pairs={{0,8},{4,12},{8,0},{12,4},{16,24},{20,28},{24,16},{28,20},{1,9},{5... | collective-permute-start | bytes 1078280 | tf_op jit(solution)/shard_map/ppermute | solution.py:481
  397.5 19.2 %collective-permute-start.39 = (bf16[104,1728]{1,0:T(8,128)(2,1)S(1)}, bf16[104,1728]{1,0:T(8,128)(2,1)S(1)}, u32[]{:S(2)}, u32[]{:S(2)}) collective-permute-start(bf16[104,1728]{1,0:T(8,128)(2,1)S(1)} %add_convert_fusion.3), channel_id=1, source_target_pairs={{0,16},{4,20},{8,24},{12,28},{16,0},{20,4},{24,8},{28,12},{1,17},{... | collective-permute-start | bytes 1078280 | tf_op jit(solution)/shard_map/ppermute | solution.py:481
  406.1 10.6 %collective-permute-start.35 = (bf16[2,104,576]{2,1,0:T(8,128)(2,1)S(1)}, bf16[2,104,576]{2,1,0:T(8,128)(2,1)S(1)}, u32[]{:S(2)}, u32[]{:S(2)}) collective-permute-start(bf16[2,104,576]{2,1,0:T(8,128)(2,1)S(1)} %get-tuple-element.295), channel_id=1, source_target_pairs={{0,16},{4,20},{8,24},{12,28},{16,0},{20,4},{24,8},{28,12},{1,17},{... | collective-permute-start | bytes 718856 | tf_op jit(solution)/shard_map/ppermute | solution.py:481
  407.8 9.3 %collective-permute-start.36 = (bf16[2,104,576]{2,1,0:T(8,128)(2,1)S(1)}, bf16[2,104,576]{2,1,0:T(8,128)(2,1)S(1)}, u32[]{:S(2)}, u32[]{:S(2)}) collective-permute-start(bf16[2,104,576]{2,1,0:T(8,128)(2,1)S(1)} %get-tuple-element.294), channel_id=1, source_target_pairs={{0,8},{4,12},{8,0},{12,4},{16,24},{20,28},{24,16},{28,20},{1,9},{5... | collective-permute-start | bytes 718856 | tf_op jit(solution)/shard_map/ppermute | solution.py:481
  407.9 12.4 %collective-permute-start.37 = (bf16[2,104,576]{2,1,0:T(8,128)(2,1)S(1)}, bf16[2,104,576]{2,1,0:T(8,128)(2,1)S(1)}, u32[]{:S(2)}, u32[]{:S(2)}) collective-permute-start(bf16[2,104,576]{2,1,0:T(8,128)(2,1)S(1)} %get-tuple-element.293), channel_id=1, source_target_pairs={{0,24},{4,28},{8,16},{12,20},{16,8},{20,12},{24,0},{28,4},{1,25},{... | collective-permute-start | bytes 718856 | tf_op jit(solution)/shard_map/ppermute | solution.py:481
  420.3 7.4 %collective-permute-start.42 = (bf16[56,1728]{1,0:T(8,128)(2,1)S(1)}, bf16[56,1728]{1,0:T(8,128)(2,1)S(1)}, u32[]{:S(2)}, u32[]{:S(2)}) collective-permute-start(bf16[56,1728]{1,0:T(8,128)(2,1)S(1)} %slice.423), channel_id=1, source_target_pairs={{0,16},{4,20},{8,24},{12,28},{16,0},{20,4},{24,8},{28,12},{1,17},{... | collective-permute-start | bytes 580616 | tf_op jit(solution)/shard_map/ppermute | solution.py:481
  422.0 5.7 %collective-permute-start.41 = (bf16[48,1728]{1,0:T(8,128)(2,1)S(1)}, bf16[48,1728]{1,0:T(8,128)(2,1)S(1)}, u32[]{:S(2)}, u32[]{:S(2)}) collective-permute-start(bf16[48,1728]{1,0:T(8,128)(2,1)S(1)} %slice.422), channel_id=1, source_target_pairs={{0,8},{4,12},{8,0},{12,4},{16,24},{20,28},{24,16},{28,20},{1,9},{5... | collective-permute-start | bytes 497672 | tf_op jit(solution)/shard_map/ppermute | solution.py:481
  422.7 5.0 %collective-permute-start.40 = (bf16[104,576]{1,0:T(8,128)(2,1)S(1)}, bf16[104,576]{1,0:T(8,128)(2,1)S(1)}, u32[]{:S(2)}, u32[]{:S(2)}) collective-permute-start(bf16[104,576]{1,0:T(8,128)(2,1)S(1)} %slice_bitcast_fusion.3), channel_id=1, source_target_pairs={{0,3},{1,0},{2,1},{3,2},{4,7},{5,4},{6,5},{7,6},{8,11},{9,8},{10,9... | collective-permute-start | bytes 359432 | tf_op jit(solution)/shard_map/ppermute | solution.py:477
  428.0 10.4 %collective-permute-start.46 = (bf16[4,104,1728]{2,1,0:T(8,128)(2,1)S(1)}, bf16[4,104,1728]{2,1,0:T(8,128)(2,1)S(1)}, u32[]{:S(2)}, u32[]{:S(2)}) collective-permute-start(bf16[4,104,1728]{2,1,0:T(8,128)(2,1)S(1)} %pad_maximum_fusion.x), channel_id=1, source_target_pairs={{0,4},{4,0},{8,12},{12,8},{16,20},{20,16},{24,28},{28,24},{1,5},{5... | collective-permute-start | bytes 4313096 | tf_op jit(solution)/shard_map/ppermute | solution.py:481
  428.1 6.2 %collective-permute-start.43 = (bf16[104,576]{1,0:T(8,128)(2,1)S(1)}, bf16[104,576]{1,0:T(8,128)(2,1)S(1)}, u32[]{:S(2)}, u32[]{:S(2)}) collective-permute-start(bf16[104,576]{1,0:T(8,128)(2,1)S(1)} %fusion.31), channel_id=1, source_target_pairs={{0,8},{4,12},{8,0},{12,4},{16,24},{20,28},{24,16},{28,20},{1,9},{5... | collective-permute-start | bytes 359432 | tf_op jit(solution)/shard_map/ppermute | solution.py:481
  429.9 8.5 %collective-permute-start.44 = (bf16[104,576]{1,0:T(8,128)(2,1)S(1)}, bf16[104,576]{1,0:T(8,128)(2,1)S(1)}, u32[]{:S(2)}, u32[]{:S(2)}) collective-permute-start(bf16[104,576]{1,0:T(8,128)(2,1)S(1)} %fusion.31), channel_id=1, source_target_pairs={{0,16},{4,20},{8,24},{12,28},{16,0},{20,4},{24,8},{28,12},{1,17},{... | collective-permute-start | bytes 359432 | tf_op jit(solution)/shard_map/ppermute | solution.py:481
  430.2 8.1 %collective-permute-start.45 = (bf16[104,576]{1,0:T(8,128)(2,1)S(1)}, bf16[104,576]{1,0:T(8,128)(2,1)S(1)}, u32[]{:S(2)}, u32[]{:S(2)}) collective-permute-start(bf16[104,576]{1,0:T(8,128)(2,1)S(1)} %fusion.31), channel_id=1, source_target_pairs={{0,24},{4,28},{8,16},{12,20},{16,8},{20,12},{24,0},{28,4},{1,25},{... | collective-permute-start | bytes 359432 | tf_op jit(solution)/shard_map/ppermute | solution.py:481
  438.5 7.8 %collective-permute-start.47 = (bf16[4,104,576]{2,1,0:T(8,128)(2,1)S(1)}, bf16[4,104,576]{2,1,0:T(8,128)(2,1)S(1)}, u32[]{:S(2)}, u32[]{:S(2)}) collective-permute-start(bf16[4,104,576]{2,1,0:T(8,128)(2,1)S(1)} %pad_maximum_fusion.2.x), channel_id=1, source_target_pairs={{0,4},{4,0},{8,12},{12,8},{16,20},{20,16},{24,28},{28,24},{1,5},{5... | collective-permute-start | bytes 1437704 | tf_op jit(solution)/shard_map/ppermute | solution.py:481
  (30 other events, 116.4 us)
